TPU v7x, 128 devices: a whole 4x4x4 slice. The times are simulated.
128 devices in a mesh: row: 16 (over y, x_hi, core), col: 8 (over z, x_lo).
Axes of the slice: x: 4 (x_hi: 2, x_lo: 2; x = x_hi * 2 + x_lo), y: 4, z: 4, core: 2. Of those that a mesh axis runs over, the one named last changes fastest.
Arguments:
- layer_input: bfloat16 [8192, 8192], P('row', 'col'), may hold values from -48 to 48
- w_query: bfloat16 [8192, 8192], P('row', 'col'), may hold values from -0.0625 to 0.0625
- w_key: bfloat16 [8192, 1024], P('row', 'col'), may hold values from -0.0625 to 0.0625
- w_value: bfloat16 [8192, 1024], P('row', 'col'), may hold values from -0.0625 to 0.0625
- counts: int32 [64], replicated, may hold values from 1 to 128
- pattern: int32 [64, 4], P('row'), may hold values from 0 to 63, as said below
- cotangent: bfloat16 [8192, 8192], P('row', 'col'), may hold values from -6 to 6
Outputs:
- attended: bfloat16 [8192, 8192], P('row', 'col')
- input_grad: bfloat16 [8192, 8192], P('row', 'col')
Inputs may be any that keep to these rules, and one draw needn't show every extreme that they name: `pattern`: row b lists 4 different blocks, b itself first; every entry lies at a cyclic distance of at most 4 blocks from b, and the second entry exactly at that distance.
All inputs are finite; a program needn't handle non-finite values.
Results may differ from a plain program's by a relative error of at most 0.035.
The roundings to bfloat16 on the way count: a program that leaves them out, or rounds other values in their place, can miss the bound.
Values may be sent and summed in bfloat16 or wider, within the bound.
A program may use at most 128 MiB of HBM per device.

v0:
```python
import jax
import jax.numpy as jnp
from jax import lax
from jax.sharding import PartitionSpec as P

HEADS = 64
KV_HEADS = 8
HEAD_DIM = 128
BLOCK = 128


def padded(block, sides, width):
    for axis, dim in sides:
        count = lax.axis_size(axis)
        forward = [(i, i + 1) for i in range(count - 1)]
        forward.append((count - 1, 0))
        backward = [(target, source) for source, target in forward]
        low = lax.ppermute(
            lax.slice_in_dim(block, block.shape[dim] - width, None, axis=dim), axis, forward
        )
        high = lax.ppermute(lax.slice_in_dim(block, 0, width, axis=dim), axis, backward)
        block = jnp.concatenate([low, block, high], axis=dim)
    return block


def shifted(block, axis, distance):
    devices = range(lax.axis_size(axis))
    route = [((i - distance) % len(devices), i) for i in devices]
    return lax.ppermute(block, axis, route)


def body(layer_input, w_query, w_key, w_value, counts, pattern, cotangent):
    score_scale = HEAD_DIM ** (-0.5)
    group_size = HEADS // KV_HEADS
    tok_rows = layer_input.shape[0]
    per_dev = tok_rows // BLOCK
    block_count = per_dev * lax.axis_size("row")
    myself = lax.axis_index("row")
    all_features = lax.all_gather(layer_input, "col", axis=1, tiled=True)
    full_query = lax.all_gather(w_query, "row", axis=0, tiled=True)
    full_key = lax.all_gather(w_key, "row", axis=0, tiled=True)
    full_value = lax.all_gather(w_value, "row", axis=0, tiled=True)
    query = jnp.dot(all_features, full_query, preferred_element_type=jnp.float32).astype(
        jnp.bfloat16
    )
    keys = jnp.dot(all_features, full_key, preferred_element_type=jnp.float32).astype(jnp.bfloat16)
    values = jnp.dot(all_features, full_value, preferred_element_type=jnp.float32).astype(
        jnp.bfloat16
    )
    kv_heads = keys.shape[1] // HEAD_DIM
    kv_cols = kv_heads * HEAD_DIM
    joined = jnp.concatenate([keys, values], axis=1)
    source = padded(joined, (("row", 0),), tok_rows)
    first_block = myself * per_dev - per_dev
    span_blocks = 3 * per_dev
    nearby = pattern.shape[1]
    local_index = jnp.mod(pattern - first_block, block_count)
    stacked = source.reshape(span_blocks, BLOCK, 2 * kv_cols)
    picked = jnp.take(stacked, local_index, axis=0).reshape(
        per_dev, nearby * BLOCK, 2, kv_heads, HEAD_DIM
    )
    key_blocks = picked[:, :, 0]
    value_blocks = picked[:, :, 1]
    positions = jnp.arange(BLOCK, dtype=jnp.int32)
    key_counts = jnp.take(counts, pattern, axis=0)
    key_live = (positions[None, None, :] < key_counts[:, :, None]).reshape(per_dev, nearby * BLOCK)
    own_counts = lax.dynamic_slice_in_dim(counts, myself * per_dev, per_dev)
    query_live = (positions[None, :] < own_counts[:, None])[:, :, None, None, None]
    query_blocks = query.reshape(per_dev, BLOCK, kv_heads, group_size, HEAD_DIM)
    scores = (
        jnp.einsum(
            "bqkgd,bjkd->bkgqj", query_blocks, key_blocks, preferred_element_type=jnp.float32
        )
        * score_scale
    )
    scores = jnp.where(key_live[:, None, None, None, :], scores, -1e30)
    score_max = jnp.max(scores, axis=-1, keepdims=True)
    exponent = jnp.exp(scores - score_max)
    prob_full = exponent / jnp.sum(exponent, axis=-1, keepdims=True)
    probs_low = prob_full.astype(jnp.bfloat16)
    mixed_out = jnp.einsum(
        "bkgqj,bjkd->bqkgd", probs_low, value_blocks, preferred_element_type=jnp.float32
    )
    attended = (mixed_out * query_live.astype(jnp.float32)).astype(jnp.bfloat16)
    grad_out = cotangent.reshape(
        per_dev, BLOCK, kv_heads, group_size, HEAD_DIM
    ) * query_live.astype(jnp.bfloat16)
    row_delta = jnp.einsum(
        "bqkgd,bqkgd->bkgq", grad_out, attended, preferred_element_type=jnp.float32
    )
    grad_probs = jnp.einsum(
        "bqkgd,bjkd->bkgqj", grad_out, value_blocks, preferred_element_type=jnp.float32
    )
    grad_scores = (prob_full * (grad_probs - row_delta[..., None]) * score_scale).astype(
        jnp.bfloat16
    )
    grad_query = jnp.einsum(
        "bkgqj,bjkd->bqkgd", grad_scores, key_blocks, preferred_element_type=jnp.float32
    )
    grad_query = grad_query.astype(jnp.bfloat16).reshape(tok_rows, -1)
    key_part = jnp.einsum(
        "bkgqj,bqkgd->bjkd", grad_scores, query_blocks, preferred_element_type=jnp.float32
    )
    value_part = jnp.einsum(
        "bkgqj,bqkgd->bjkd", probs_low, grad_out, preferred_element_type=jnp.float32
    )
    grad_parts = jnp.concatenate(
        [
            key_part.reshape(per_dev * nearby, BLOCK, kv_cols),
            value_part.reshape(per_dev * nearby, BLOCK, kv_cols),
        ],
        axis=-1,
    )
    owed_grads = (
        jnp.zeros((span_blocks, BLOCK, 2 * kv_cols), jnp.float32)
        .at[local_index.reshape(-1)]
        .add(grad_parts)
    )
    from_next = shifted(owed_grads[:per_dev].astype(jnp.bfloat16), "row", -1).astype(jnp.float32)
    from_prev = shifted(owed_grads[2 * per_dev :].astype(jnp.bfloat16), "row", 1).astype(
        jnp.float32
    )
    settled = owed_grads[per_dev : 2 * per_dev] + from_next + from_prev
    settled = settled.reshape(tok_rows, 2 * kv_cols)
    grad_keys = settled[:, :kv_cols].astype(jnp.bfloat16)
    grad_values = settled[:, kv_cols:].astype(jnp.bfloat16)
    contract = (((1,), (1,)), ((), ()))
    partial_grad = lax.dot_general(
        grad_query, full_query, contract, preferred_element_type=jnp.float32
    )
    partial_grad = partial_grad + lax.dot_general(
        grad_keys, full_key, contract, preferred_element_type=jnp.float32
    )
    partial_grad = partial_grad + lax.dot_general(
        grad_values, full_value, contract, preferred_element_type=jnp.float32
    )
    input_grad = lax.psum_scatter(
        partial_grad.astype(jnp.bfloat16), "col", scatter_dimension=1, tiled=True
    )
    return (attended.reshape(tok_rows, -1), input_grad)


def solution(mesh):
    placed = (
        P("row", "col"),
        P("row", "col"),
        P("row", "col"),
        P("row", "col"),
        P(),
        P("row", None),
        P("row", "col"),
    )
    return jax.shard_map(
        body,
        mesh=mesh,
        in_specs=placed,
        out_specs=(P("row", "col"), P("row", "col")),
        check_vma=False,
    )
```

profile of v0, /device:TPU:10, one launch (start us, length us, event | category | flops | bytes accessed | tf_op | source)
XLA Modules:
  0.0 667.0 jit_solution(15478223276111546973)
XLA Ops:
  7.2 0.7 all-gather.9.cloned.1.call-update
  7.9 0.0 all-gather.5.cloned.1.call-start
  7.9 0.7 all-gather.5.cloned.1.call-update
  8.6 0.0 all-gather.7.cloned.1.call-start
  8.7 0.7 all-gather.7.cloned.1.call-update
  9.4 0.0 all-gather.11.cloned.1.call-start
  9.4 0.5 all-gather.11.cloned.1.call-update
  10.0 0.0 reduce-scatter.2.cloned.1.call-start
  10.0 0.7 compare_select_fusion
  10.7 0.1 reshape.230
  10.8 0.7 compare_and_fusion
  11.5 0.1 reshape.215
  11.6 0.1 reshape.222
  11.7 0.7 dynamic_slice.3
  12.4 1.3 gather_fusion.1
  13.7 0.1 reshape.229
  13.8 0.1 broadcast_bitcast_fusion.1
  13.9 0.1 fusion.36
  14.0 0.7 and_select_fusion
  14.6 0.1 broadcast_bitcast_fusion
  14.7 44.3 %all-gather.9.cloned.1.call-done = bf16[8192,128]{1,0:T(8,128)(2,1)} async-done(((bf16[512,128]{1,0:T(8,128)(2,1)}), bf16[8192,128]{1,0:T(8,128)(2,1)}) %all-gather.9.cloned.1.call-update) | async-done | bytes 2097168 | tf_op jit(solution)/shard_map/all_gather | solution.py:42
  59.0 170.1 %all-gather.5.cloned.1.call-done = bf16[512,8192]{1,0:T(8,128)(2,1)} async-done(((bf16[512,1024]{1,0:T(8,128)(2,1)}), bf16[512,8192]{1,0:T(8,128)(2,1)}) %all-gather.5.cloned.1.call-update) | async-done | bytes 8388624 | tf_op jit(solution)/shard_map/all_gather | solution.py:39
  229.1 6.9 %convolution_convert_fusion.2 = bf16[512,128]{0,1:T(8,128)(2,1)S(1)} fusion(bf16[512,8192]{1,0:T(8,128)(2,1)} %all-gather.5.cloned.1.call-done, bf16[8192,128]{1,0:T(8,128)(2,1)} %all-gather.9.cloned.1.call-done), kind=kOutput, calls=%fused_computation.31 | convolution fusion | flops 1073807360 | bytes 10616832 | tf_op jit(solution)/shard_map/dot_general | solution.py:47
  236.0 42.9 %all-gather.7.cloned.1.call-done = bf16[8192,128]{1,0:T(8,128)(2,1)} async-done(((bf16[512,128]{1,0:T(8,128)(2,1)}), bf16[8192,128]{1,0:T(8,128)(2,1)}) %all-gather.7.cloned.1.call-update) | async-done | bytes 2097168 | tf_op jit(solution)/shard_map/all_gather | solution.py:41
  278.8 6.9 %convolution_convert_fusion.3 = bf16[512,128]{0,1:T(8,128)(2,1)S(1)} fusion(bf16[512,8192]{1,0:T(8,128)(2,1)} %all-gather.5.cloned.1.call-done, bf16[8192,128]{1,0:T(8,128)(2,1)} %all-gather.7.cloned.1.call-done), kind=kOutput, calls=%fused_computation.32 | convolution fusion | flops 1073807360 | bytes 10616832 | tf_op jit(solution)/shard_map/dot_general | solution.py:46
  285.7 1.6 collective-permute-start.1
  287.4 0.3 copy.63
  287.7 1.6 copy.25
  289.3 3.8 collective-permute-done.1
  293.2 6.9 %collective-permute-done = bf16[512,256]{0,1:T(8,128)(2,1)S(1)} collective-permute-done((bf16[512,256]{0,1:T(8,128)(2,1)S(1)}, bf16[512,256]{0,1:T(8,128)(2,1)S(1)}, u32[]{:S(2)}, u32[]{:S(2)}) %collective-permute-start) | collective-permute-done | bytes 262176 | tf_op jit(solution)/shard_map/ppermute | solution.py:18
  300.1 0.1 pad_maximum_fusion.1
  300.1 0.3 copy.19
  300.4 0.6 gather_fusion
  301.0 0.3 gather.11
  301.3 0.5 copy_select_fusion
  301.8 88.8 %all-gather.11.cloned.1.call-done = bf16[8192,1024]{1,0:T(8,128)(2,1)} async-done(((bf16[512,1024]{1,0:T(8,128)(2,1)}), bf16[8192,1024]{1,0:T(8,128)(2,1)}) %all-gather.11.cloned.1.call-update) | async-done | bytes 16777232 | tf_op jit(solution)/shard_map/all_gather | solution.py:40
  390.6 14.8 %fusion.16 = bf16[64,8,8,128]{3,1,2,0:T(8,128)(2,1)S(1)} fusion(bf16[512,8192]{1,0:T(8,128)(2,1)} %all-gather.5.cloned.1.call-done, bf16[8192,1024]{1,0:T(8,128)(2,1)} %all-gather.11.cloned.1.call-done), kind=kOutput, calls=%fused_computation.27 | convolution fusion | flops 8590458880 | bytes 26214400 | tf_op jit(solution)/shard_map/dot_general | solution.py:43
  405.4 0.3 copy.61
  405.7 1.9 bitcast_reduce_fusion
  407.6 1.9 fusion.5
  409.5 4.3 fusion.18
  413.8 4.0 fusion.12
  417.8 3.7 fusion.6
  421.5 2.0 copy-done
  423.5 1.8 fusion.17
  425.2 8.0 %copy.49 = bf16[4,8,128,512]{3,1,2,0:T(8,128)(2,1)} copy(bf16[4,8,128,512]{2,3,1,0:T(8,128)(2,1)} %copy-done) | data formatting | bytes 8388608 | tf_op jit(solution)/shard_map/reshape.34
  433.2 0.3 copy.34
  433.6 3.1 convolution_bitcast_fusion
  436.6 0.3 copy.32
  437.0 2.4 copy.29
  439.4 1.5 pad_maximum_fusion
  440.8 0.1 broadcast_in_dim.52
  441.0 3.5 scatter_fusion
  444.5 0.1 convert.8
  444.6 0.7 fusion.42
  445.3 2.7 collective-permute-start.2
  448.0 15.7 %fusion.21 = f32[512,8192]{1,0:T(8,128)} fusion(bf16[8192,1024]{1,0:T(8,128)(2,1)} %all-gather.11.cloned.1.call-done, bf16[64,8,8,128]{3,2,1,0:T(8,128)(2,1)S(1)} %bitcast.184), kind=kOutput, calls=%fused_computation.33 | convolution fusion | flops 8589934592 | bytes 34603008 | tf_op jit(solution)/shard_map/dot_general | solution.py:128
  463.8 0.1 fusion.29
  463.9 9.8 %fusion.33 = f32[512,8192]{1,0:T(8,128)} fusion(bf16[8192,128]{1,0:T(8,128)(2,1)} %all-gather.7.cloned.1.call-done, bf16[512,256]{1,0:T(8,128)(2,1)S(1)} %bitcast.180), kind=kOutput, calls=%fused_computation.52 | convolution fusion | flops 1073741824 | bytes 19005440 | tf_op jit(solution)/shard_map/dot_general | solution.py:131
  473.7 15.3 %add_convert_fusion = bf16[512,8192]{1,0:T(8,128)(2,1)} fusion(f32[512,8192]{1,0:T(8,128)} %fusion.21, f32[512,8192]{1,0:T(8,128)} %fusion.33, bf16[8192,128]{1,0:T(8,128)(2,1)S(1)} %copy-done.1, bf16[512,256]{1,0:T(8,128)(2,1)S(1)} %bitcast.181), kind=kOutput, calls=%fused_computation.3 | convolution fusion | flops 1086324736 | bytes 44171264 | tf_op jit(solution)/shard_map/dot_general | solution.py:134
  489.0 1.2 copy-done.3
  490.2 0.7 copy.24
  490.9 1.2 copy.77
  492.2 168.3 %reduce-scatter.2.cloned.1.call-done = bf16[512,1024]{1,0:T(8,128)(2,1)} async-done(((bf16[512,8192]{1,0:T(8,128)(2,1)}), bf16[512,1024]{1,0:T(8,128)(2,1)}) %reduce-scatter.2.cloned.1.call-update) | async-done | bytes 1048592 | tf_op jit(solution)/shard_map/reduce_scatter | solution.py:137
  (26 shorter events, 0.1 us)
Async XLA Ops:
  7.2 51.8 %all-gather.9.cloned.1.call-start = ((), (), s32[]{:S(2)}) async-start(), calls=%async_computation.3 | async-start | bytes 2228224 | tf_op jit(solution)/shard_map/all_gather | solution.py:42
  7.9 221.2 %all-gather.5.cloned.1.call-start = ((), (), s32[]{:S(2)}) async-start(), calls=%async_computation.1 | async-start | bytes 9437184 | tf_op jit(solution)/shard_map/all_gather | solution.py:39
  8.6 270.2 %all-gather.7.cloned.1.call-start = ((), (), s32[]{:S(2)}) async-start(), calls=%async_computation.2 | async-start | bytes 2228224 | tf_op jit(solution)/shard_map/all_gather | solution.py:41
  9.4 381.2 %all-gather.11.cloned.1.call-start = ((), (), s32[]{:S(2)}) async-start(), calls=%async_computation.4 | async-start | bytes 17825792 | tf_op jit(solution)/shard_map/all_gather | solution.py:40
  10.0 650.5 %reduce-scatter.2.cloned.1.call-start = ((), (), s32[]{:S(2)}) async-start(), calls=%async_computation.5 | async-start | bytes 9437184 | tf_op jit(solution)/shard_map/reduce_scatter | solution.py:137
  14.7 272.7 %copy-start.2 = (bf16[512,1024]{1,0:T(8,128)(2,1)S(1)}, bf16[512,1024]{1,0:T(8,128)(2,1)}, u32[]{:S(2)}) copy-start(bf16[512,1024]{1,0:T(8,128)(2,1)} %param.13) | copy-start | bytes 3145732
  285.7 7.4 %collective-permute-start.1 = (bf16[512,256]{0,1:T(8,128)(2,1)S(1)}, bf16[512,256]{0,1:T(8,128)(2,1)S(1)}, u32[]{:S(2)}, u32[]{:S(2)}) collective-permute-start(bf16[512,256]{0,1:T(8,128)(2,1)S(1)} %pad_maximum_fusion.2), channel_id=1, source_target_pairs={{8,0},{16,8},{24,16},{32,24},{40,32},{48,40},{56,48},{64,56},{72,6... | collective-permute-start | bytes 786440 | tf_op jit(solution)/shard_map/ppermute | solution.py:21
  287.4 12.7 %collective-permute-start = (bf16[512,256]{0,1:T(8,128)(2,1)S(1)}, bf16[512,256]{0,1:T(8,128)(2,1)S(1)}, u32[]{:S(2)}, u32[]{:S(2)}) collective-permute-start(bf16[512,256]{0,1:T(8,128)(2,1)S(1)} %pad_maximum_fusion.2), channel_id=1, source_target_pairs={{0,8},{8,16},{16,24},{24,32},{32,40},{40,48},{48,56},{56,64},{64,7... | collective-permute-start | bytes 786440 | tf_op jit(solution)/shard_map/ppermute | solution.py:18
  405.6 3.9 copy-start.4
  421.5 2.0 copy-start
  425.2 8.0 %copy-start.6 = (f32[4,512,1,128]{1,3,0,2:T(8,128)S(1)}, f32[4,512,1,128]{1,3,0,2:T(8,128)}, u32[]{:S(2)}) copy-start(f32[4,512,1,128]{1,3,0,2:T(8,128)} %fusion.18) | copy-start | bytes 3145732
  440.8 7.2 %copy-start.5 = (bf16[4,128,1,8,128]{4,3,1,0,2:T(8,128)(2,1)S(1)}, bf16[4,128,1,8,128]{4,3,1,0,2:T(8,128)(2,1)}, u32[]{:S(2)}) copy-start(bf16[4,128,1,8,128]{4,3,1,0,2:T(8,128)(2,1)} %copy.29) | copy-start | bytes 3145732
  445.3 18.4 %collective-permute-start.2 = (bf16[4,128,256]{2,1,0:T(8,128)(2,1)}, bf16[4,128,256]{2,1,0:T(8,128)(2,1)S(1)}, u32[]{:S(2)}, u32[]{:S(2)}) collective-permute-start(bf16[4,128,256]{2,1,0:T(8,128)(2,1)} %get-tuple-element.4), channel_id=1, source_target_pairs={{8,0},{16,8},{24,16},{32,24},{40,32},{48,40},{56,48},{64,56},{72,6... | collective-permute-start | bytes 786440 | tf_op jit(solution)/shard_map/ppermute | solution.py:29
  448.0 15.7 %collective-permute-start.3 = (bf16[4,128,256]{2,1,0:T(8,128)(2,1)S(1)}, bf16[4,128,256]{2,1,0:T(8,128)(2,1)S(1)}, u32[]{:S(2)}, u32[]{:S(2)}) collective-permute-start(bf16[4,128,256]{2,1,0:T(8,128)(2,1)S(1)} %get-tuple-element.5), channel_id=1, source_target_pairs={{120,0},{0,8},{8,16},{16,24},{24,32},{32,40},{40,48},{48,56},{56,6... | collective-permute-start | bytes 786440 | tf_op jit(solution)/shard_map/ppermute | solution.py:29
  463.8 9.8 %copy-start.1 = (bf16[8192,128]{1,0:T(8,128)(2,1)S(1)}, bf16[8192,128]{1,0:T(8,128)(2,1)}, u32[]{:S(2)}) copy-start(bf16[8192,128]{1,0:T(8,128)(2,1)} %all-gather.9.cloned.1.call-done) | copy-start | bytes 6291460
  489.0 1.2 copy-start.3
Sparse Core Ops, SparseCore 0:
  10.5 48.5 all-gather.8
  60.7 168.4 all-gather.4
  231.6 47.2 all-gather.6
  281.2 109.3 all-gather.10
  489.1 171.3 reduce-scatter.1
where the time goes:
time: 668 us; the launch traced here: 667 us
  waiting for transfers between devices  528 us (79%)
  matrix products  88 us (13%)
  local copies, waits for them, and re-layouts  22.9 us (3%)
  between operations  14 us (2%)
  other arithmetic  9.82 us (1%)
    all_gather x1, waiting for transfers between devices, body(): all_features = lax.all_gather(layer_input, 'col', axis=1, tiled=True)  170 us
    reduce_scatter x1, waiting for transfers between devices, body(): lax.psum_scatter(partial_grad.astype(jnp.bfloat16), 'col', scatter_dimens...  168 us
    all_gather x1, waiting for transfers between devices, body(): full_query = lax.all_gather(w_query, 'row', axis=0, tiled=True)  88.8 us
    all_gather x1, waiting for transfers between devices, body(): full_value = lax.all_gather(w_value, 'row', axis=0, tiled=True)  44.3 us
    all_gather x1, waiting for transfers between devices, body(): full_key = lax.all_gather(w_key, 'row', axis=0, tiled=True)  42.9 us
    dot_general x1, matrix products, body(): lax.dot_general(grad_query, full_query, contract, preferred_element_type=...  15.7 us
    dot_general x1, matrix products, body(): lax.dot_general(grad_values, full_value, contract, preferred_element_type...  15.3 us
    dot_general x1, matrix products, body(): jnp.dot(all_features, full_query, preferred_element_type=jnp.float32)  14.8 us
  transfers between devices with their start and end apart: 9, of which 7 were waited for; matrix products, arithmetic and copies ran while one was open for 6% of the time, Pallas kernels for 0%

commit v1 on v0

--- a/solution.py
+++ b/solution.py
@@ -1,26 +1,290 @@
+import functools
+
 import jax
 import jax.numpy as jnp
 from jax import lax
+from jax.experimental import pallas as pl
+from jax.experimental.pallas import tpu as pltpu
 from jax.sharding import PartitionSpec as P
 
 HEADS = 64
 KV_HEADS = 8
 HEAD_DIM = 128
 BLOCK = 128
-
-
-def padded(block, sides, width):
-    for axis, dim in sides:
-        count = lax.axis_size(axis)
-        forward = [(i, i + 1) for i in range(count - 1)]
-        forward.append((count - 1, 0))
-        backward = [(target, source) for source, target in forward]
-        low = lax.ppermute(
-            lax.slice_in_dim(block, block.shape[dim] - width, None, axis=dim), axis, forward
-        )
-        high = lax.ppermute(lax.slice_in_dim(block, 0, width, axis=dim), axis, backward)
-        block = jnp.concatenate([low, block, high], axis=dim)
-    return block
+GROUP = HEADS // KV_HEADS
+ROWS = 16
+COLS = 8
+TOK = 512
+HALF = 256
+FEAT = 1024
+KV = 256
+WIDE = FEAT + KV
+MESH = pl.DeviceIdType.MESH
+MIB = 1024 * 1024
+
+
+def place():
+    row, col = lax.axis_index("row"), lax.axis_index("col")
+    return row, col, row // 4, (row // 2) % 2, row % 2, col // 2, col % 2
+
+
+def remote(src, dst, send, recv, row, col):
+    return pltpu.make_async_remote_copy(
+        src_ref=src,
+        dst_ref=dst,
+        send_sem=send,
+        recv_sem=recv,
+        device_id=(row, col),
+        device_id_type=MESH,
+    )
+
+
+BRINGS = {0: (3, 0), 1: (3, 1), 2: (1, 1), 3: (1, 0), 4: (2, 0), 5: (2, 1)}
+
+
+def gather_kernel(
+    x_in, wq_in, wk_in, wv_in,
+    q_out, kv_out, w_out,
+    xf, wf, acc, kv_buf,
+    load_sem, xs, xr, xps, xpr, ws, wr, wps, wpr, cs, cr, hs, hr, out_sem, kv_sem,
+):
+    row, col, y, h, k, z, l = place()
+    prev_row, next_row = (row + ROWS - 1) % ROWS, (row + 1) % ROWS
+
+    def row_of(yy, hh, kk):
+        return (yy * 2 + hh) * 2 + kk
+
+    y_next, y_prev = row_of((y + 1) % 4, h, k), row_of((y + 3) % 4, h, k)
+    h_pair, sibling = row_of(y, 1 - h, k), row_of(y, h, 1 - k)
+    z_next, z_prev = ((z + 1) % 4) * 2 + l, ((z + 3) % 4) * 2 + l
+    l_pair = z * 2 + 1 - l
+
+    own_x, own_w = col, row // 2
+    own_rows = pl.ds(k * TOK, TOK)
+    loads = [
+        pltpu.make_async_copy(x_in, xf.at[own_x], load_sem.at[0]),
+        pltpu.make_async_copy(wq_in, wf.at[own_w, own_rows, pl.ds(0, FEAT)], load_sem.at[1]),
+        pltpu.make_async_copy(wk_in, wf.at[own_w, own_rows, pl.ds(FEAT, 128)], load_sem.at[2]),
+        pltpu.make_async_copy(
+            wv_in, wf.at[own_w, own_rows, pl.ds(FEAT + 128, 128)], load_sem.at[3]
+        ),
+    ]
+    for load in loads:
+        load.start()
+
+    barrier = pltpu.get_barrier_semaphore()
+    peers = [
+        (row, z_next), (row, z_prev), (row, l_pair),
+        (y_next, col), (y_prev, col), (h_pair, col), (sibling, col),
+        (prev_row, col), (next_row, col),
+    ]
+    for peer in peers:
+        pl.semaphore_signal(barrier, inc=1, device_id=peer, device_id_type=MESH)
+    pl.semaphore_wait(barrier, len(peers))
+    for load in loads:
+        load.wait()
+
+    def x_piece(step, plane, half):
+        slot = ((z + step) % 4) * 2 + (l + plane) % 2
+        return xf.at[slot, pl.ds(half * HALF, HALF)]
+
+    def w_piece(step, plane, half, core=None):
+        slot = ((y + step) % 4) * 2 + (h + plane) % 2
+        core = k if core is None else core
+        return wf.at[slot, pl.ds(core * TOK + half * HALF, HALF)]
+
+    started = []
+
+    def x_ring(plane, kind):
+        step, half = (0, (0, 1, 1, 0)[kind]) if kind < 4 else ((3, 0) if kind == 4 else (1, 1))
+        ref = x_piece(step, plane, half)
+        peer = z_next if kind in (0, 1, 4) else z_prev
+        i = plane * 6 + kind
+        copy = remote(ref, ref, xs.at[i], xr.at[i], row, peer)
+        copy.start()
+        started.append(copy)
+
+    def x_got(plane, kind):
+        step, half = BRINGS[kind]
+        ref = x_piece(step, plane, half)
+        i = plane * 6 + kind
+        remote(ref, ref, xs.at[i], xr.at[i], row, z_prev).wait_recv()
+
+    def w_ring(plane, kind):
+        step, half = (0, (0, 1, 1, 0)[kind]) if kind < 4 else ((3, 0) if kind == 4 else (1, 1))
+        ref = w_piece(step, plane, half)
+        peer = y_next if kind in (0, 1, 4) else y_prev
+        i = plane * 6 + kind
+        copy = remote(ref, ref, ws.at[i], wr.at[i], peer, col)
+        copy.start()
+        started.append(copy)
+
+    def w_share(step, plane, half):
+        ref = w_piece(step, plane, half)
+        i = (step * 2 + plane) * 2 + half
+        copy = remote(ref, ref, cs.at[i], cr.at[i], sibling, col)
+        copy.start()
+        started.append(copy)
+
+    def w_shared(step, plane, half):
+        ref = w_piece(step, plane, half, 1 - k)
+        i = (step * 2 + plane) * 2 + half
+        remote(ref, ref, cs.at[i], cr.at[i], sibling, col).wait_recv()
+
+    def w_got(plane, kind):
+        step, half = BRINGS[kind]
+        ref = w_piece(step, plane, half)
+        i = plane * 6 + kind
+        remote(ref, ref, ws.at[i], wr.at[i], y_prev, col).wait_recv()
+        if kind in (0, 2):
+            w_ring(plane, 4 if kind == 0 else 5)
+        w_share(step, plane, half)
+
+    for kind in (0, 2, 1, 3):
+        x_ring(0, kind)
+        w_ring(0, kind)
+    for half in range(2):
+        ref = x_piece(0, 0, half)
+        copy = remote(ref, ref, xps.at[half], xpr.at[half], row, l_pair)
+        copy.start()
+        started.append(copy)
+        ref = w_piece(0, 0, half)
+        copy = remote(ref, ref, wps.at[half], wpr.at[half], h_pair, col)
+        copy.start()
+        started.append(copy)
+        w_share(0, 0, half)
+
+    for kind in (0, 2):
+        x_got(0, kind)
+        x_ring(0, 4 if kind == 0 else 5)
+        w_got(0, kind)
+    for half in range(2):
+        ref = x_piece(0, 1, half)
+        remote(ref, ref, xps.at[half], xpr.at[half], row, l_pair).wait_recv()
+        for kind in ((0, 3), (1, 2))[half]:
+            x_ring(1, kind)
+        ref = w_piece(0, 1, half)
+        remote(ref, ref, wps.at[half], wpr.at[half], h_pair, col).wait_recv()
+        for kind in ((0, 3), (1, 2))[half]:
+            w_ring(1, kind)
+        w_share(0, 1, half)
+    for kind in (1, 3, 4, 5):
+        x_got(0, kind)
+        w_got(0, kind)
+    for kind in (0, 2):
+        x_got(1, kind)
+        x_ring(1, 4 if kind == 0 else 5)
+        w_got(1, kind)
+    for kind in (1, 3):
+        x_got(1, kind)
+        w_got(1, kind)
+    for step in (0, 1, 3):
+        for plane in range(2):
+            for half in range(2):
+                w_shared(step, plane, half)
+    for half in range(2):
+        w_shared(2, 0, half)
+
+    late_x = ((z + 2) % 4) * 2 + 1 - l
+    late_w = ((y + 2) % 4) * 2 + 1 - h
+
+    def multiply(slot, tile):
+        cols = pl.ds(pl.multiple_of(tile * 256, 256), 256)
+        return jnp.dot(xf[slot], wf[slot, :, cols], preferred_element_type=jnp.float32)
+
+    @pl.loop(0, WIDE // 256)
+    def _(tile):
+        acc[tile] = jnp.zeros((TOK, 256), jnp.float32)
+
+    for slot in range(COLS):
+        @pl.when((slot != late_x) & (slot != late_w))
+        def _():
+            @pl.loop(0, WIDE // 256)
+            def _(tile):
+                acc[tile] += multiply(slot, tile)
+
+        @pl.when(slot != late_w)
+        def _():
+            pltpu.make_async_copy(wf.at[slot], w_out.at[slot], out_sem.at[slot]).start()
+
+    for kind in (4, 5):
+        x_got(1, kind)
+        w_got(1, kind)
+    for half in range(2):
+        w_shared(2, 1, half)
+    for slot in range(COLS):
+        @pl.when(slot == late_w)
+        def _():
+            pltpu.make_async_copy(wf.at[slot], w_out.at[slot], out_sem.at[slot]).start()
+
+    def finish(tile):
+        acc[tile] += multiply(late_x, tile)
+
+        @pl.when(late_w != late_x)
+        def _():
+            acc[tile] += multiply(late_w, tile)
+
+        return acc[tile].astype(jnp.bfloat16)
+
+    kv_buf[...] = finish(FEAT // 256)
+    halo = [
+        remote(kv_buf, kv_out.at[0], hs.at[0], hr.at[0], next_row, col),
+        remote(kv_buf, kv_out.at[2], hs.at[1], hr.at[1], prev_row, col),
+    ]
+    for copy in halo:
+        copy.start()
+    own_kv = pltpu.make_async_copy(kv_buf, kv_out.at[1], kv_sem)
+    own_kv.start()
+
+    @pl.loop(0, FEAT // 256)
+    def _(tile):
+        cols = pl.ds(pl.multiple_of(tile * 256, 256), 256)
+        q_out[:, cols] = finish(tile)
+
+    for copy in started:
+        copy.wait_send()
+    for copy in halo:
+        copy.wait()
+    own_kv.wait()
+    for slot in range(COLS):
+        pltpu.make_async_copy(wf.at[slot], w_out.at[slot], out_sem.at[slot]).wait()
+
+
+def gather(layer_input, w_query, w_key, w_value):
+    dma = pltpu.SemaphoreType.DMA
+    return pl.pallas_call(
+        gather_kernel,
+        name="gather_project",
+        out_shape=(
+            jax.ShapeDtypeStruct((TOK, FEAT), jnp.bfloat16),
+            jax.ShapeDtypeStruct((3, TOK, KV), jnp.bfloat16),
+            jax.ShapeDtypeStruct((COLS, FEAT, WIDE), jnp.bfloat16),
+        ),
+        in_specs=[pl.BlockSpec(memory_space=pl.ANY)] * 4,
+        out_specs=(
+            pl.BlockSpec(memory_space=pltpu.VMEM),
+            pl.BlockSpec(memory_space=pl.ANY),
+            pl.BlockSpec(memory_space=pl.ANY),
+        ),
+        scratch_shapes=[
+            pltpu.VMEM((COLS, TOK, FEAT), jnp.bfloat16),
+            pltpu.VMEM((COLS, FEAT, WIDE), jnp.bfloat16),
+            pltpu.VMEM((WIDE // 256, TOK, 256), jnp.float32),
+            pltpu.VMEM((TOK, KV), jnp.bfloat16),
+            dma((4,)),
+            dma((12,)), dma((12,)), dma((2,)), dma((2,)),
+            dma((12,)), dma((12,)), dma((2,)), dma((2,)),
+            dma((16,)), dma((16,)),
+            dma((2,)), dma((2,)),
+            dma((COLS,)), dma,
+        ],
+        compiler_params=pltpu.CompilerParams(
+            collective_id=0, has_side_effects=True, vmem_limit_bytes=56 * MIB
+        ),
+        cost_estimate=pl.CostEstimate(
+            flops=2 * TOK * 8192 * WIDE, bytes_accessed=40 * MIB, transcendentals=0
+        ),
+    )(layer_input, w_query, w_key, w_value)
 
 
 def shifted(block, axis, distance):
@@ -36,21 +300,9 @@
     per_dev = tok_rows // BLOCK
     block_count = per_dev * lax.axis_size("row")
     myself = lax.axis_index("row")
-    all_features = lax.all_gather(layer_input, "col", axis=1, tiled=True)
-    full_query = lax.all_gather(w_query, "row", axis=0, tiled=True)
-    full_key = lax.all_gather(w_key, "row", axis=0, tiled=True)
-    full_value = lax.all_gather(w_value, "row", axis=0, tiled=True)
-    query = jnp.dot(all_features, full_query, preferred_element_type=jnp.float32).astype(
-        jnp.bfloat16
-    )
-    keys = jnp.dot(all_features, full_key, preferred_element_type=jnp.float32).astype(jnp.bfloat16)
-    values = jnp.dot(all_features, full_value, preferred_element_type=jnp.float32).astype(
-        jnp.bfloat16
-    )
-    kv_heads = keys.shape[1] // HEAD_DIM
-    kv_cols = kv_heads * HEAD_DIM
-    joined = jnp.concatenate([keys, values], axis=1)
-    source = padded(joined, (("row", 0),), tok_rows)
+    query, source, full_wide = gather(layer_input, w_query, w_key, w_value)
+    kv_heads = 1
+    kv_cols = 128
     first_block = myself * per_dev - per_dev
     span_blocks = 3 * per_dev
     nearby = pattern.shape[1]
@@ -125,14 +377,9 @@
     grad_keys = settled[:, :kv_cols].astype(jnp.bfloat16)
     grad_values = settled[:, kv_cols:].astype(jnp.bfloat16)
     contract = (((1,), (1,)), ((), ()))
+    joined = jnp.concatenate([grad_query, grad_keys, grad_values], axis=1)
     partial_grad = lax.dot_general(
-        grad_query, full_query, contract, preferred_element_type=jnp.float32
-    )
-    partial_grad = partial_grad + lax.dot_general(
-        grad_keys, full_key, contract, preferred_element_type=jnp.float32
-    )
-    partial_grad = partial_grad + lax.dot_general(
-        grad_values, full_value, contract, preferred_element_type=jnp.float32
+        joined, full_wide.reshape(-1, WIDE), contract, preferred_element_type=jnp.float32
     )
     input_grad = lax.psum_scatter(
         partial_grad.astype(jnp.bfloat16), "col", scatter_dimension=1, tiled=True

time: 668 us -> 377 us (0.56)
  waiting for transfers between devices: 528 us -> 170 us
  Pallas kernels: 0 us -> 106 us
  matrix products: 88 us -> 42.2 us
    all_gather x4 -> x0, waiting for transfers between devices: 346 us -> none  [the longest x1 170 us: body(): all_features = lax.all_gather(layer_input, 'col', axis=1, tiled=True)]
    pallas_call x0 -> x1, Pallas kernels: none -> 106 us  [gather(): pl.pallas_call(gather_kernel, name='gather_project', out_shape=(jax.Shape...]
    dot_general x6 -> x1, matrix products: 69.3 us -> 17.5 us  [body(): lax.dot_general(joined, full_wide.reshape(-1, WIDE), contract, preferred_...]
    ppermute x2 -> x0, waiting for transfers between devices: 10.7 us -> none  [the longest x1 6.91 us: padded(): lax.ppermute(lax.slice_in_dim(block, block.shape[dim] - width, None, axis...]
  transfers between devices with their start and end apart: 9 -> 3, of which waited for: 7 -> 2; matrix products, arithmetic and copies ran while one was open for 6% -> 2% of each run, Pallas kernels for 0% -> 0%
where the time goes in v1:
time: 377 us; the launch traced here: 376 us
  waiting for transfers between devices  170 us (45%)
  Pallas kernels  106 us (28%)
  matrix products  42.2 us (11%)
  local copies, waits for them, and re-layouts  28.3 us (8%)
  between operations  14.2 us (4%)
  other arithmetic  12 us (3%)
    reduce_scatter x1, waiting for transfers between devices, body(): lax.psum_scatter(partial_grad.astype(jnp.bfloat16), 'col', scatter_dimens...  166 us
    pallas_call x1, Pallas kernels, gather(): pl.pallas_call(gather_kernel, name='gather_project', out_shape=(jax.Shape...  106 us
    dot_general x1, matrix products, body(): lax.dot_general(joined, full_wide.reshape(-1, WIDE), contract, preferred_...  17.5 us
    unnamed x15, local copies, waits for them, and re-layouts  8.19 us
    another operation x1, local copies, waits for them, and re-layouts  7.94 us
  transfers between devices with their start and end apart: 3, of which 2 were waited for; matrix products, arithmetic and copies ran while one was open for 2% of the time, Pallas kernels for 0%

profile of v1, /device:TPU:10, one launch (start us, length us, event | category | flops | bytes accessed | tf_op | source)
XLA Modules:
  0.0 375.6 jit_solution(6956864332141953820)
XLA Ops:
  7.2 0.0 reduce-scatter.2.cloned.1.call-start
  7.2 0.7 compare_select_fusion
  7.9 0.7 compare_and_fusion
  8.6 0.1 reshape.218
  8.7 0.1 reshape.234
  8.8 0.1 reshape.226
  8.9 0.1 broadcast_bitcast_fusion.1
  9.0 0.7 dynamic_slice.3
  9.7 0.1 fusion.32
  9.8 1.3 gather_fusion.1
  11.1 0.1 reshape.233
  11.2 0.7 and_select_fusion
  11.9 0.1 broadcast_bitcast_fusion
  11.9 1.5 copy.62
  13.4 1.5 copy.24
  14.9 106.3 %gather_project.1 = (bf16[512,1024]{1,0:T(8,128)(2,1)}, bf16[3,512,256]{2,1,0:T(8,128)(2,1)}, bf16[8,1024,1280]{2,1,0:T(8,128)(2,1)}) custom-call(bf16[512,1024]{1,0:T(8,128)(2,1)} %x_in.1, bf16[512,1024]{1,0:T(8,128)(2,1)} %wq_in.1, bf16[512,128]{1,0:T(8,128)(2,1)} %wk_in.1, bf16[512,128]{1,0:T(8,128)(2,1)} %wv_in.1), custom_call_target="tpu_custom_call" | custom-call | flops 10737418240 | bytes 41943040 | tf_op jit(solution)/shard_map/gather_project/pallas_call | solution.py:255
  121.2 1.5 copy.60
  122.7 1.8 gather_fusion
  124.4 0.3 gather.11
  124.8 0.5 copy_select_fusion
  125.2 0.0 copy-start.3
  125.2 1.9 bitcast_reduce_fusion
  127.1 0.0 copy-start
  127.1 1.9 fusion.5
  129.1 1.3 copy-done
  130.4 0.0 copy-done.3
  130.4 4.2 %fusion.17 = f32[4,512,1,128]{1,3,0,2:T(8,128)} fusion(bf16[4,128,8,128]{1,3,2,0:T(8,128)(2,1)S(1)} %copy-done.3, bf16[4,128]{1,0:T(4,128)(2,1)S(1)} %get-tuple-element.12, f32[4,8,128]{2,1,0:T(8,128)S(1)} %fusion.5, f32[4,8,128]{2,1,0:T(8,128)S(1)} %get-tuple-element.14, f32[4,512,128,8]{2,1,3,0:T(8,128)S(1)} %get-tuple-element.15, ...), kind=kOutput, calls=%fused_computation.27 | convolution fusion | flops 547880960 | bytes 10521600 | tf_op jit(solution)/shard_map/bkgqj,bqkgd->bjkd/dot_general | solution.py:356
  134.6 2.6 copy.33
  137.2 0.0 copy-start.1
  137.2 6.6 %fusion.12 = (f32[4,8,128]{2,1,0:T(8,128)S(1)}, bf16[4,1,128,8,128]{4,2,3,0,1:T(8,128)(2,1)}) fusion(bf16[4,128,8,128]{1,3,2,0:T(8,128)(2,1)S(1)} %copy-done.3, bf16[4,128]{1,0:T(4,128)(2,1)S(1)} %get-tuple-element.12, f32[4,128]{1,0:T(4,128)S(1)} %get-tuple-element.13, f32[4,8,128]{2,1,0:T(8,128)S(1)} %fusion.5, f32[4,8,128]{2,1,0:T(8,128)S(1)} %get-tuple-element.14, ...), kind=kOutput, calls=%fused_computation.22 | convolution fusion | flops 551022592 | bytes 11064320 | tf_op jit(solution)/shard_map/bkgqj,bjkd->bqkgd/dot_general | solution.py:333
  143.8 0.0 copy-done.1
  143.8 5.1 %fusion.6 = bf16[4,8,128,512]{2,3,1,0:T(8,128)(2,1)} fusion(f32[4,8,128]{2,1,0:T(8,128)S(1)} %get-tuple-element.16, f32[4,8,128]{2,1,0:T(8,128)S(1)} %fusion.5, f32[4,8,128]{2,1,0:T(8,128)S(1)} %get-tuple-element.14, f32[4,512,128,8]{2,1,3,0:T(8,128)S(1)} %copy-done.1, pred[4,512]{1,0:T(4,128)(4,1)S(1)} %bitcast_compare_fusion, ...), kind=kOutput, calls=%fused_computation.14 | convolution fusion | flops 555745280 | bytes 14208000 | tf_op jit(solution)/shard_map/bqkgd,bjkd->bkgqj/dot_general | solution.py:343
  148.9 7.9 %copy.48 = bf16[4,8,128,512]{3,1,2,0:T(8,128)(2,1)} copy(bf16[4,8,128,512]{2,3,1,0:T(8,128)(2,1)} %fusion.6) | data formatting | bytes 8388608 | tf_op jit(solution)/shard_map/reshape.35
  156.8 3.0 convolution_bitcast_fusion
  159.9 0.3 copy.31
  160.2 2.8 pad_maximum_fusion
  163.0 0.1 broadcast_in_dim.52
  163.1 3.5 scatter_fusion
  166.6 0.1 convert.8
  166.7 0.9 fusion.39
  167.6 2.4 collective-permute-start
  170.0 0.0 collective-permute-start.1
  170.0 3.9 %fusion.16 = bf16[4,128,1,8,128]{1,4,3,0,2:T(8,128)(2,1)} fusion(bf16[4,8,128,512]{2,3,1,0:T(8,128)(2,1)} %fusion.6, bf16[4,512,2,1,128]{4,1,0,3,2:T(8,128)(2,1)S(1)} %copy_select_fusion), kind=kOutput, calls=%fused_computation.26 | convolution fusion | flops 537395200 | bytes 5767168 | tf_op jit(solution)/shard_map/bkgqj,bjkd->bqkgd/dot_general | solution.py:349
  173.9 1.7 copy.28
  175.6 1.2 copy.73
  176.8 0.0 collective-permute-done
  176.8 4.1 %collective-permute-done.1 = bf16[4,128,256]{2,1,0:T(8,128)(2,1)} collective-permute-done((bf16[4,128,256]{2,1,0:T(8,128)(2,1)}, bf16[4,128,256]{2,1,0:T(8,128)(2,1)}, u32[]{:S(2)}, u32[]{:S(2)}) %collective-permute-start.1) | collective-permute-done | bytes 262176 | tf_op jit(solution)/shard_map/ppermute | solution.py:293
  180.9 1.0 fusion.28
  181.9 17.5 %convolution_convert_fusion = bf16[512,8192]{1,0:T(8,128)(2,1)} fusion(bf16[8192,1280]{1,0:T(8,128)(2,1)} %bitcast.180, bf16[512,256]{1,0:T(8,128)(2,1)S(1)} %bitcast.178, bf16[512,1024]{1,0:T(8,128)(2,1)} %bitcast.175), kind=kOutput, calls=%fused_computation.3 | convolution fusion | flops 10744233984 | bytes 30670848 | tf_op jit(solution)/shard_map/dot_general | solution.py:381
  199.4 0.0 copy-start.2
  199.4 0.0 reduce-scatter.2.cloned.1.call-update
  199.5 1.2 copy-done.2
  200.7 0.7 copy.23
  201.4 1.2 copy.74
  202.6 166.1 %reduce-scatter.2.cloned.1.call-done = bf16[512,1024]{1,0:T(8,128)(2,1)} async-done(((bf16[512,8192]{1,0:T(8,128)(2,1)}), bf16[512,1024]{1,0:T(8,128)(2,1)}) %reduce-scatter.2.cloned.1.call-update) | async-done | bytes 1048592 | tf_op jit(solution)/shard_map/reduce_scatter | solution.py:384
  (7 shorter events, 0.0 us)
Async XLA Ops:
  7.2 361.6 %reduce-scatter.2.cloned.1.call-start = ((), (), s32[]{:S(2)}) async-start(), calls=%async_computation.1 | async-start | bytes 9437184 | tf_op jit(solution)/shard_map/reduce_scatter | solution.py:384
  125.2 5.2 %copy-start.3 = (bf16[4,128,8,128]{1,3,2,0:T(8,128)(2,1)S(1)}, bf16[4,128,8,128]{1,3,2,0:T(8,128)(2,1)}, u32[]{:S(2)}) copy-start(bf16[4,128,8,128]{1,3,2,0:T(8,128)(2,1)} %copy.24) | copy-start | bytes 3145732
  127.1 3.3 copy-start
  137.2 6.6 %copy-start.1 = (f32[4,512,128,8]{2,1,3,0:T(8,128)S(1)}, f32[4,512,128,8]{2,1,3,0:T(8,128)}, u32[]{:S(2)}) copy-start(f32[4,512,128,8]{2,1,3,0:T(8,128)} %copy-done) | copy-start | bytes 25165828
  167.6 9.2 %collective-permute-start = (bf16[4,128,256]{2,1,0:T(8,128)(2,1)}, bf16[4,128,256]{2,1,0:T(8,128)(2,1)S(1)}, u32[]{:S(2)}, u32[]{:S(2)}) collective-permute-start(bf16[4,128,256]{2,1,0:T(8,128)(2,1)} %get-tuple-element.10), channel_id=1, source_target_pairs={{8,0},{16,8},{24,16},{32,24},{40,32},{48,40},{56,48},{64,56},{72,6... | collective-permute-start | bytes 786440 | tf_op jit(solution)/shard_map/ppermute | solution.py:293
  170.0 10.9 %collective-permute-start.1 = (bf16[4,128,256]{2,1,0:T(8,128)(2,1)}, bf16[4,128,256]{2,1,0:T(8,128)(2,1)}, u32[]{:S(2)}, u32[]{:S(2)}) collective-permute-start(bf16[4,128,256]{2,1,0:T(8,128)(2,1)} %get-tuple-element.11), channel_id=1, source_target_pairs={{120,0},{0,8},{8,16},{16,24},{24,32},{32,40},{40,48},{48,56},{56,6... | collective-permute-start | bytes 786440 | tf_op jit(solution)/shard_map/ppermute | solution.py:293
  199.4 1.2 copy-start.2
Sparse Core Ops, SparseCore 0:
  199.6 169.1 reduce-scatter.1

commit v2 on v1

--- a/solution.py
+++ b/solution.py
@@ -287,10 +287,204 @@
     )(layer_input, w_query, w_key, w_value)
 
 
-def shifted(block, axis, distance):
-    devices = range(lax.axis_size(axis))
-    route = [((i - distance) % len(devices), i) for i in devices]
-    return lax.ppermute(block, axis, route)
+def scatter_kernel(
+    dq_in, side_in, mid_in, w_in,
+    out,
+    jn, wv, acc, pb, far, near, pair_out, pair_in, side_got,
+    w_sem, ds, dr, fs, fr, ns, nr, ps, pr,
+):
+    row, col, y, h, k, z, l = place()
+    prev_row, next_row = (row + ROWS - 1) % ROWS, (row + 1) % ROWS
+    z_next, z_prev = ((z + 1) % 4) * 2 + l, ((z + 3) % 4) * 2 + l
+    l_pair = z * 2 + 1 - l
+
+    def slot_of(step, plane):
+        return ((z + step) % 4) * 2 + (l + plane) % 2
+
+    order = [(2, 1), (1, 1), (3, 1), (2, 0), (1, 0), (3, 0), (0, 1), (0, 0)]
+    loads = {}
+    for i, (step, plane) in enumerate(order):
+        slot = slot_of(step, plane)
+        loads[step, plane] = pltpu.make_async_copy(w_in.at[slot], wv.at[slot], w_sem.at[i])
+        loads[step, plane].start()
+
+    barrier = pltpu.get_barrier_semaphore()
+    peers = [(row, z_next), (row, z_prev), (row, l_pair), (prev_row, col), (next_row, col)]
+    for peer in peers:
+        pl.semaphore_signal(barrier, inc=1, device_id=peer, device_id_type=MESH)
+    jn[:, :FEAT] = dq_in[...]
+    pl.semaphore_wait(barrier, len(peers))
+
+    started = []
+
+    def send(src, dst, send_sem, recv_sem, to_row, to_col):
+        copy = remote(src, dst, send_sem, recv_sem, to_row, to_col)
+        copy.start()
+        started.append(copy)
+
+    def got(ref, send_sem, recv_sem):
+        remote(ref, ref, send_sem, recv_sem, row, z_prev).wait_recv()
+
+    send(side_in.at[0], side_got.at[1], ds.at[0], dr.at[0], prev_row, col)
+    send(side_in.at[1], side_got.at[0], ds.at[1], dr.at[1], next_row, col)
+
+    def product(slot, tile, rows, cols):
+        tall = pl.ds(pl.multiple_of(tile * 256, 256), 256)
+        return lax.dot_general(
+            jn[rows, cols], wv[slot, tall, cols], (((1,), (1,)), ((), ())),
+            preferred_element_type=jnp.float32,
+        )
+
+    every = pl.ds(0, WIDE)
+
+    def fill(target, step, plane, rows, extra=None):
+        slot = slot_of(step, plane)
+
+        @pl.loop(0, FEAT // 256)
+        def _(tile):
+            cols = pl.ds(pl.multiple_of(tile * 256, 256), 256)
+            value = product(slot, tile, rows, every)
+            if extra is not None:
+                value += extra[:, cols].astype(jnp.float32)
+            target[rows, cols] = value.astype(jnp.bfloat16)
+
+    low, high = pl.ds(0, HALF), pl.ds(HALF, HALF)
+    both = pl.ds(0, TOK)
+
+    loads[2, 1].wait()
+
+    @pl.loop(0, FEAT // 256)
+    def _(tile):
+        acc[tile] = product(slot_of(2, 1), tile, both, pl.ds(0, FEAT))
+
+    for i in range(2):
+        got(side_got.at[1 - i], ds.at[i], dr.at[i])
+    jn[:, FEAT:] = (
+        mid_in[...] + side_got[0].astype(jnp.float32) + side_got[1].astype(jnp.float32)
+    ).astype(jnp.bfloat16)
+
+    @pl.loop(0, FEAT // 256)
+    def _(tile):
+        cols = pl.ds(pl.multiple_of(tile * 256, 256), 256)
+        value = acc[tile] + product(slot_of(2, 1), tile, both, pl.ds(FEAT, KV))
+        pb[1, 0, :, cols] = value.astype(jnp.bfloat16)
+
+    def send_far(plane):
+        i = plane * 2
+        send(pb.at[plane, 0, low], far.at[plane, 0], fs.at[i], fr.at[i], row, z_next)
+        send(pb.at[plane, 0, high], far.at[plane, 1], fs.at[i + 1], fr.at[i + 1], row, z_prev)
+
+    def near_half(plane, way, half, extra=None):
+        step = 1 if way == 0 else 3
+        rows = low if half == 0 else high
+        fill(pb.at[plane, 1 + way], step, plane, rows, extra)
+        i = (plane * 2 + way) * 2 + half
+        send(
+            pb.at[plane, 1 + way, rows], near.at[plane, way, rows], ns.at[i], nr.at[i],
+            row, z_next if way == 0 else z_prev,
+        )
+
+    def near_free(plane):
+        near_half(plane, 0, 1)
+        near_half(plane, 1, 0)
+
+    def near_joined(plane):
+        i = plane * 2
+        got(far.at[plane, 0], fs.at[i], fr.at[i])
+        near_half(plane, 0, 0, far.at[plane, 0])
+        got(far.at[plane, 1], fs.at[i + 1], fr.at[i + 1])
+        near_half(plane, 1, 1, far.at[plane, 1])
+
+    send_far(1)
+    loads[1, 1].wait()
+    loads[3, 1].wait()
+    near_free(1)
+    loads[2, 0].wait()
+    fill(pb.at[0, 0], 2, 0, both)
+    send_far(0)
+    near_joined(1)
+    loads[1, 0].wait()
+    loads[3, 0].wait()
+    near_free(0)
+    near_joined(0)
+
+    def own(plane):
+        loads[0, plane].wait()
+
+        @pl.loop(0, FEAT // 256)
+        def _(tile):
+            acc[tile] = product(slot_of(0, plane), tile, both, every)
+
+    def near_wait(plane, half):
+        rows = low if half == 0 else high
+        for way in range(2):
+            i = (plane * 2 + way) * 2 + half
+            got(near.at[plane, way, rows], ns.at[i], nr.at[i])
+
+    own(1)
+    for half in range(2):
+        near_wait(1, half)
+        rows = low if half == 0 else high
+
+        @pl.loop(0, FEAT // 256)
+        def _(tile):
+            cols = pl.ds(pl.multiple_of(tile * 256, 256), 256)
+            value = acc[tile, rows] + near[1, 0, rows, cols].astype(jnp.float32)
+            value += near[1, 1, rows, cols].astype(jnp.float32)
+            pair_out[rows, cols] = value.astype(jnp.bfloat16)
+
+        send(pair_out.at[rows], pair_in.at[rows], ps.at[half], pr.at[half], row, l_pair)
+    own(0)
+    for half in range(2):
+        near_wait(0, half)
+        rows = low if half == 0 else high
+        got(pair_in.at[rows], ps.at[half], pr.at[half])
+
+        @pl.loop(0, FEAT // 256)
+        def _(tile):
+            cols = pl.ds(pl.multiple_of(tile * 256, 256), 256)
+            value = acc[tile, rows] + near[0, 0, rows, cols].astype(jnp.float32)
+            value += near[0, 1, rows, cols].astype(jnp.float32)
+            value += pair_in[rows, cols].astype(jnp.float32)
+            out[rows, cols] = value.astype(jnp.bfloat16)
+
+    for copy in started:
+        copy.wait_send()
+
+
+def scatter(grad_query, side, mid, full_wide):
+    dma = pltpu.SemaphoreType.DMA
+    vmem = pl.BlockSpec(memory_space=pltpu.VMEM)
+    low = jnp.bfloat16
+    return pl.pallas_call(
+        scatter_kernel,
+        name="project_scatter",
+        out_shape=jax.ShapeDtypeStruct((TOK, FEAT), low),
+        in_specs=[vmem, vmem, vmem, pl.BlockSpec(memory_space=pl.ANY)],
+        out_specs=vmem,
+        scratch_shapes=[
+            pltpu.VMEM((TOK, WIDE), low),
+            pltpu.VMEM((COLS, FEAT, WIDE), low),
+            pltpu.VMEM((FEAT // 256, TOK, 256), jnp.float32),
+            pltpu.VMEM((2, 3, TOK, FEAT), low),
+            pltpu.VMEM((2, 2, HALF, FEAT), low),
+            pltpu.VMEM((2, 2, TOK, FEAT), low),
+            pltpu.VMEM((TOK, FEAT), low),
+            pltpu.VMEM((TOK, FEAT), low),
+            pltpu.VMEM((2, TOK, KV), low),
+            dma((COLS,)),
+            dma((2,)), dma((2,)),
+            dma((4,)), dma((4,)),
+            dma((8,)), dma((8,)),
+            dma((2,)), dma((2,)),
+        ],
+        compiler_params=pltpu.CompilerParams(
+            collective_id=1, has_side_effects=True, vmem_limit_bytes=56 * MIB
+        ),
+        cost_estimate=pl.CostEstimate(
+            flops=2 * TOK * 8192 * WIDE, bytes_accessed=24 * MIB, transcendentals=0
+        ),
+    )(grad_query, side, mid, full_wide)
 
 
 def body(layer_input, w_query, w_key, w_value, counts, pattern, cotangent):
@@ -368,22 +562,10 @@
         .at[local_index.reshape(-1)]
         .add(grad_parts)
     )
-    from_next = shifted(owed_grads[:per_dev].astype(jnp.bfloat16), "row", -1).astype(jnp.float32)
-    from_prev = shifted(owed_grads[2 * per_dev :].astype(jnp.bfloat16), "row", 1).astype(
-        jnp.float32
-    )
-    settled = owed_grads[per_dev : 2 * per_dev] + from_next + from_prev
-    settled = settled.reshape(tok_rows, 2 * kv_cols)
-    grad_keys = settled[:, :kv_cols].astype(jnp.bfloat16)
-    grad_values = settled[:, kv_cols:].astype(jnp.bfloat16)
-    contract = (((1,), (1,)), ((), ()))
-    joined = jnp.concatenate([grad_query, grad_keys, grad_values], axis=1)
-    partial_grad = lax.dot_general(
-        joined, full_wide.reshape(-1, WIDE), contract, preferred_element_type=jnp.float32
-    )
-    input_grad = lax.psum_scatter(
-        partial_grad.astype(jnp.bfloat16), "col", scatter_dimension=1, tiled=True
-    )
+    side = jnp.stack([owed_grads[:per_dev], owed_grads[2 * per_dev :]])
+    side = side.astype(jnp.bfloat16).reshape(2, TOK, KV)
+    mid = owed_grads[per_dev : 2 * per_dev].reshape(TOK, KV)
+    input_grad = scatter(grad_query, side, mid, full_wide)
     return (attended.reshape(tok_rows, -1), input_grad)
 
 

time: 377 us -> 256 us (0.68)
  waiting for transfers between devices: 170 us -> 0 us
  Pallas kernels: 106 us -> 193 us
  matrix products: 42.2 us -> 21.5 us
  between operations: 14.2 us -> 0.87 us
    reduce_scatter x1 -> x0, waiting for transfers between devices: 166 us -> none  [body(): lax.psum_scatter(partial_grad.astype(jnp.bfloat16), 'col', scatter_dimens...]
    pallas_call x0 -> x1, Pallas kernels: none -> 87.1 us  [scatter(): pl.pallas_call(scatter_kernel, name='project_scatter', out_shape=jax.Shap...]
    dot_general x1 -> x0, matrix products: 17.5 us -> none  [body(): lax.dot_general(joined, full_wide.reshape(-1, WIDE), contract, preferred_...]
    ppermute x2 -> x0, waiting for transfers between devices: 4.07 us -> none  [shifted(): return lax.ppermute(block, axis, route)]
    unnamed x15 -> x16, local copies, waits for them, and re-layouts: 8.19 us -> 9.86 us
  transfers between devices with their start and end apart: 3 -> 0, of which waited for: 2 -> 0; matrix products, arithmetic and copies ran while one was open for 2% -> 0% of each run, Pallas kernels for 0% -> 0%
where the time goes in v2:
time: 256 us; the launch traced here: 254 us
  Pallas kernels  193 us (75%)
  local copies, waits for them, and re-layouts  27.7 us (11%)
  matrix products  21.5 us (8%)
  other arithmetic  10.1 us (4%)
    pallas_call x1, Pallas kernels, gather(): pl.pallas_call(gather_kernel, name='gather_project', out_shape=(jax.Shape...  106 us
    pallas_call x1, Pallas kernels, scatter(): pl.pallas_call(scatter_kernel, name='project_scatter', out_shape=jax.Shap...  87.1 us
    unnamed x16, local copies, waits for them, and re-layouts  9.86 us
    another operation x1, local copies, waits for them, and re-layouts  7.94 us
    dot_general x1, matrix products, body(): jnp.einsum('bqkgd,bjkd->bkgqj', grad_out, value_blocks, preferred_element...  6.4 us
    dot_general x1, matrix products, body(): jnp.einsum('bkgqj,bqkgd->bjkd', probs_low, grad_out, preferred_element_ty...  5.41 us

profile of v2, /device:TPU:10, one launch (start us, length us, event | category | flops | bytes accessed | tf_op | source)
XLA Modules:
  0.0 253.5 jit_solution(9001795241990941671)
XLA Ops:
  0.6 1.5 copy.63
  2.1 1.5 copy.25
  3.6 0.7 dynamic_slice.3
  4.3 0.1 fusion.27
  4.4 0.7 compare_select_fusion
  5.1 0.1 reshape.236
  5.2 1.3 gather_fusion.1
  6.5 0.1 reshape.235
  6.6 0.7 and_select_fusion
  7.3 0.1 broadcast_bitcast_fusion
  7.3 0.0 copy-start.3
  7.4 106.2 %gather_project.1 = (bf16[512,1024]{1,0:T(8,128)(2,1)}, bf16[3,512,256]{2,1,0:T(8,128)(2,1)}, bf16[8,1024,1280]{2,1,0:T(8,128)(2,1)}) custom-call(bf16[512,1024]{1,0:T(8,128)(2,1)} %x_in.1, bf16[512,1024]{1,0:T(8,128)(2,1)} %wq_in.1, bf16[512,128]{1,0:T(8,128)(2,1)} %wk_in.1, bf16[512,128]{1,0:T(8,128)(2,1)} %wv_in.1), custom_call_target="tpu_custom_call" | custom-call | flops 10737418240 | bytes 41943040 | tf_op jit(solution)/shard_map/gather_project/pallas_call | solution.py:255
  113.6 1.5 copy.61
  115.1 0.0 copy-done.3
  115.1 0.1 reshape.228
  115.2 1.7 gather_fusion
  117.0 0.3 gather.11
  117.3 0.1 broadcast_bitcast_fusion.1
  117.4 0.5 copy_select_fusion
  117.9 0.0 copy-start.2
  117.9 1.9 bitcast_reduce_fusion
  119.8 0.0 copy-start
  119.8 1.9 fusion.5
  121.7 0.0 copy-done.2
  121.7 4.0 %fusion.12 = (f32[4,8,128]{2,1,0:T(8,128)S(1)}, bf16[4,1,128,8,128]{4,2,3,0,1:T(8,128)(2,1)}) fusion(bf16[4,128,8,128]{1,3,2,0:T(8,128)(2,1)S(1)} %copy-done.2, bf16[4,128]{1,0:T(4,128)(2,1)S(1)} %get-tuple-element.12, f32[4,128]{1,0:T(4,128)S(1)} %get-tuple-element.13, f32[4,8,128]{2,1,0:T(8,128)S(1)} %fusion.5, f32[4,8,128]{2,1,0:T(8,128)S(1)} %get-tuple-element.14, ...), kind=kOutput, calls=%fused_computation.21 | convolution fusion | flops 551022592 | bytes 11064320 | tf_op jit(solution)/shard_map/bkgqj,bjkd->bqkgd/dot_general | solution.py:527
  125.7 0.0 copy-done
  125.7 1.7 copy.24
  127.4 1.2 copy.75
  128.7 6.4 %fusion.6 = bf16[4,8,128,512]{2,3,1,0:T(8,128)(2,1)S(1)} fusion(f32[4,8,128]{2,1,0:T(8,128)S(1)} %get-tuple-element.16, f32[4,8,128]{2,1,0:T(8,128)S(1)} %fusion.5, f32[4,8,128]{2,1,0:T(8,128)S(1)} %get-tuple-element.14, f32[4,512,128,8]{2,1,3,0:T(8,128)} %copy-done, pred[4,512]{1,0:T(4,128)(4,1)S(1)} %bitcast_compare_fusion, ...), kind=kOutput, calls=%fused_computation.13 | convolution fusion | flops 555745280 | bytes 14208000 | tf_op jit(solution)/shard_map/bqkgd,bjkd->bkgqj/dot_general | solution.py:537
  135.1 0.0 copy-start.1
  135.1 1.9 copy-done.1
  137.0 0.8 fusion.16
  137.8 0.7 copy.29
  138.5 1.3 copy.74
  139.8 0.1 reshape.222
  139.9 5.4 %fusion.17 = f32[4,512,1,128]{1,3,0,2:T(8,128)S(1)} fusion(bf16[4,128,8,128]{1,3,2,0:T(8,128)(2,1)} %copy.25, bf16[4,128]{1,0:T(4,128)(2,1)S(1)} %get-tuple-element.12, f32[4,8,128]{2,1,0:T(8,128)S(1)} %fusion.5, f32[4,8,128]{2,1,0:T(8,128)S(1)} %get-tuple-element.14, f32[4,512,128,8]{2,1,3,0:T(8,128)} %copy-done, pred[4,512]{1,0:T(4,128)(4,1)S(1)} %bitcast_compare_fusion), kind=kOutput, calls=%fused_computation.26 | convolution fusion | flops 547880960 | bytes 10521600 | tf_op jit(solution)/shard_map/bkgqj,bqkgd->bjkd/dot_general | solution.py:550
  145.3 0.3 copy.34
  145.6 7.9 %copy.49 = bf16[4,8,128,512]{3,1,2,0:T(8,128)(2,1)} copy(bf16[4,8,128,512]{2,3,1,0:T(8,128)(2,1)} %copy-done.1) | data formatting | bytes 8388608 | tf_op jit(solution)/shard_map/reshape.35
  153.6 3.1 %convolution_bitcast_fusion = f32[4,512,1,128]{1,3,0,2:T(8,128)S(1)} fusion(bf16[4,8,128,512]{3,1,2,0:T(8,128)(2,1)} %copy.49, bf16[4,128,8,128]{3,2,1,0:T(8,128)(2,1)S(1)} %bitcast.166), kind=kOutput, calls=%fused_computation.27 | convolution fusion | flops 536870912 | bytes 6291456 | tf_op jit(solution)/shard_map/bkgqj,bqkgd->bjkd/dot_general | solution.py:547
  156.6 0.3 copy.32
  157.0 1.5 pad_maximum_fusion
  158.5 0.1 broadcast_in_dim.52
  158.6 3.7 %scatter_fusion = f32[12,128,256]{2,1,0:T(8,128)S(1)} fusion(f32[12,128,256]{2,1,0:T(8,128)S(1)} %broadcast_in_dim.52, s32[16]{0:T(128)S(1)} %fusion.29, f32[16,128,256]{2,1,0:T(8,128)} %pad_maximum_fusion), kind=kCustom, calls=%fused_computation.2 | custom fusion | flops 524288 | bytes 6291520 | tf_op jit(solution)/shard_map/scatter-add | solution.py:563
  162.3 0.1 convert.8
  162.5 0.8 pad_maximum_fusion.1.side_in
  163.3 0.8 slice.30
  164.2 87.1 %project_scatter.1 = bf16[512,1024]{1,0:T(8,128)(2,1)} custom-call(bf16[512,1024]{1,0:T(8,128)(2,1)} %bitcast.175, bf16[2,512,256]{2,1,0:T(8,128)(2,1)} %pad_maximum_fusion.1.side_in, f32[512,256]{1,0:T(8,128)} %bitcast.180, bf16[8,1024,1280]{2,1,0:T(8,128)(2,1)} %get-tuple-element.7.w_in), custom_call_target="tpu_custom_call" | custom-call | flops 10737418240 | bytes 25165824 | tf_op jit(solution)/shard_map/project_scatter/pallas_call | solution.py:459
  251.3 2.3 copy.79
  (9 shorter events, 0.1 us)
Async XLA Ops:
  7.3 107.8 %copy-start.3 = (s32[4,4]{1,0:T(4,128)S(1)}, s32[4,4]{1,0:T(4,128)}, u32[]{:S(2)}) copy-start(s32[4,4]{1,0:T(4,128)} %param.12) | copy-start | bytes 196
  117.9 3.9 %copy-start.2 = (bf16[4,128,8,128]{1,3,2,0:T(8,128)(2,1)S(1)}, bf16[4,128,8,128]{1,3,2,0:T(8,128)(2,1)}, u32[]{:S(2)}) copy-start(bf16[4,128,8,128]{1,3,2,0:T(8,128)(2,1)} %copy.25) | copy-start | bytes 3145732
  119.8 6.0 %copy-start = (f32[4,512,128,8]{2,1,3,0:T(8,128)}, f32[4,512,128,8]{2,1,3,0:T(8,128)S(1)}, u32[]{:S(2)}) copy-start(f32[4,512,128,8]{2,1,3,0:T(8,128)S(1)} %get-tuple-element.15) | copy-start | bytes 25165828
  135.1 1.9 copy-start.1

commit v3 on v2

--- a/solution.py
+++ b/solution.py
@@ -487,86 +487,117 @@
     )(grad_query, side, mid, full_wide)
 
 
+def attend_kernel(
+    pattern, counts, q_in, cot_in, kv_in,
+    out, dq_out, side_out, mid_out,
+    owed,
+):
+    block = pl.program_id(0)
+    per_dev = TOK // BLOCK
+    block_count = ROWS * per_dev
+    first = lax.axis_index("row") * per_dev
+    scale = HEAD_DIM ** (-0.5)
+    pair = 2 * HEAD_DIM
+
+    @pl.when(block == 0)
+    def _():
+        owed[...] = jnp.zeros_like(owed)
+
+    chosen = [pattern[block, i] for i in range(4)]
+    local = [(b - first + per_dev + block_count) % block_count for b in chosen]
+    keys = jnp.concatenate([kv_in[i, :, :HEAD_DIM] for i in local], axis=0)
+    values = jnp.concatenate([kv_in[i, :, HEAD_DIM:] for i in local], axis=0)
+    keys_t, values_t = keys.T, values.T
+    spot = lax.broadcasted_iota(jnp.int32, (BLOCK, pair), 0)
+    live = jnp.concatenate([spot < counts[b] for b in chosen], axis=0)
+    own_count = counts[first + block]
+    lane = lax.broadcasted_iota(jnp.int32, (HEAD_DIM, pair), 1)
+    query_live = jnp.where(lane % BLOCK < own_count, 1.0, 0.0)
+    row_live = lax.broadcasted_iota(jnp.int32, (BLOCK, HEAD_DIM), 0) < own_count
+    row_live = jnp.where(row_live, 1.0, 0.0).astype(jnp.bfloat16)
+
+    def heads(ref, start, mask=None):
+        parts = [ref[:, start + i * HEAD_DIM : start + (i + 1) * HEAD_DIM] for i in range(2)]
+        if mask is not None:
+            parts = [part * mask for part in parts]
+        return jnp.concatenate(parts, axis=0)
+
+    def dot(a, b, dims):
+        return lax.dot_general(a, b, (dims, ((), ())), preferred_element_type=jnp.float32)
+
+    def put(ref, start, both):
+        low = both.astype(jnp.bfloat16)
+        for i in range(2):
+            cols = slice(start + i * HEAD_DIM, start + (i + 1) * HEAD_DIM)
+            ref[:, cols] = low[:, i * HEAD_DIM : (i + 1) * HEAD_DIM].T
+
+    grad_keys = grad_values = None
+    for start in range(0, FEAT, pair):
+        query = heads(q_in, start)
+        grad_out = heads(cot_in, start, row_live)
+        raw = jnp.where(live, dot(keys, query, ((1,), (1,))), -1e30)
+        top = jnp.max(raw, axis=0, keepdims=True)
+        power = jnp.exp((raw - top) * scale)
+        probs = power * (1.0 / jnp.sum(power, axis=0, keepdims=True))
+        probs_low = probs.astype(jnp.bfloat16)
+        put(out, start, dot(values_t, probs_low, ((1,), (0,))) * query_live)
+        grad_probs = dot(values, grad_out, ((1,), (1,)))
+        delta = jnp.sum(probs_low.astype(jnp.float32) * grad_probs, axis=0, keepdims=True)
+        grad_scores = (probs * (grad_probs - delta) * scale).astype(jnp.bfloat16)
+        put(dq_out, start, dot(keys_t, grad_scores, ((1,), (0,))))
+        key_part = dot(grad_scores, query, ((1,), (0,)))
+        value_part = dot(probs_low, grad_out, ((1,), (0,)))
+        grad_keys = key_part if grad_keys is None else grad_keys + key_part
+        grad_values = value_part if grad_values is None else grad_values + value_part
+
+    for i, spot in enumerate(local):
+        rows = slice(i * BLOCK, (i + 1) * BLOCK)
+        owed[spot, :, :HEAD_DIM] += grad_keys[rows]
+        owed[spot, :, HEAD_DIM:] += grad_values[rows]
+
+    @pl.when(block == per_dev - 1)
+    def _():
+        for i in range(per_dev):
+            rows = slice(i * BLOCK, (i + 1) * BLOCK)
+            side_out[0, rows] = owed[i].astype(jnp.bfloat16)
+            mid_out[rows] = owed[per_dev + i]
+            side_out[1, rows] = owed[2 * per_dev + i].astype(jnp.bfloat16)
+
+
+def attend(pattern, counts, query, cotangent, source):
+    per_dev = TOK // BLOCK
+    tokens = pl.BlockSpec((BLOCK, FEAT), lambda b: (b, 0))
+    smem = pl.BlockSpec(memory_space=pltpu.SMEM)
+    low = jnp.bfloat16
+    return pl.pallas_call(
+        attend_kernel,
+        name="attend",
+        grid=(per_dev,),
+        out_shape=(
+            jax.ShapeDtypeStruct((TOK, FEAT), low),
+            jax.ShapeDtypeStruct((TOK, FEAT), low),
+            jax.ShapeDtypeStruct((2, TOK, KV), low),
+            jax.ShapeDtypeStruct((TOK, KV), jnp.float32),
+        ),
+        in_specs=[
+            smem, smem, tokens, tokens,
+            pl.BlockSpec((3 * per_dev, BLOCK, KV), lambda b: (0, 0, 0)),
+        ],
+        out_specs=(
+            tokens, tokens,
+            pl.BlockSpec((2, TOK, KV), lambda b: (0, 0, 0)),
+            pl.BlockSpec((TOK, KV), lambda b: (0, 0)),
+        ),
+        scratch_shapes=[pltpu.VMEM((3 * per_dev, BLOCK, KV), jnp.float32)],
+        compiler_params=pltpu.CompilerParams(vmem_limit_bytes=40 * MIB),
+    )(pattern, counts, query, cotangent, source.reshape(3 * per_dev, BLOCK, KV))
+
+
 def body(layer_input, w_query, w_key, w_value, counts, pattern, cotangent):
-    score_scale = HEAD_DIM ** (-0.5)
-    group_size = HEADS // KV_HEADS
-    tok_rows = layer_input.shape[0]
-    per_dev = tok_rows // BLOCK
-    block_count = per_dev * lax.axis_size("row")
-    myself = lax.axis_index("row")
     query, source, full_wide = gather(layer_input, w_query, w_key, w_value)
-    kv_heads = 1
-    kv_cols = 128
-    first_block = myself * per_dev - per_dev
-    span_blocks = 3 * per_dev
-    nearby = pattern.shape[1]
-    local_index = jnp.mod(pattern - first_block, block_count)
-    stacked = source.reshape(span_blocks, BLOCK, 2 * kv_cols)
-    picked = jnp.take(stacked, local_index, axis=0).reshape(
-        per_dev, nearby * BLOCK, 2, kv_heads, HEAD_DIM
-    )
-    key_blocks = picked[:, :, 0]
-    value_blocks = picked[:, :, 1]
-    positions = jnp.arange(BLOCK, dtype=jnp.int32)
-    key_counts = jnp.take(counts, pattern, axis=0)
-    key_live = (positions[None, None, :] < key_counts[:, :, None]).reshape(per_dev, nearby * BLOCK)
-    own_counts = lax.dynamic_slice_in_dim(counts, myself * per_dev, per_dev)
-    query_live = (positions[None, :] < own_counts[:, None])[:, :, None, None, None]
-    query_blocks = query.reshape(per_dev, BLOCK, kv_heads, group_size, HEAD_DIM)
-    scores = (
-        jnp.einsum(
-            "bqkgd,bjkd->bkgqj", query_blocks, key_blocks, preferred_element_type=jnp.float32
-        )
-        * score_scale
-    )
-    scores = jnp.where(key_live[:, None, None, None, :], scores, -1e30)
-    score_max = jnp.max(scores, axis=-1, keepdims=True)
-    exponent = jnp.exp(scores - score_max)
-    prob_full = exponent / jnp.sum(exponent, axis=-1, keepdims=True)
-    probs_low = prob_full.astype(jnp.bfloat16)
-    mixed_out = jnp.einsum(
-        "bkgqj,bjkd->bqkgd", probs_low, value_blocks, preferred_element_type=jnp.float32
-    )
-    attended = (mixed_out * query_live.astype(jnp.float32)).astype(jnp.bfloat16)
-    grad_out = cotangent.reshape(
-        per_dev, BLOCK, kv_heads, group_size, HEAD_DIM
-    ) * query_live.astype(jnp.bfloat16)
-    row_delta = jnp.einsum(
-        "bqkgd,bqkgd->bkgq", grad_out, attended, preferred_element_type=jnp.float32
-    )
-    grad_probs = jnp.einsum(
-        "bqkgd,bjkd->bkgqj", grad_out, value_blocks, preferred_element_type=jnp.float32
-    )
-    grad_scores = (prob_full * (grad_probs - row_delta[..., None]) * score_scale).astype(
-        jnp.bfloat16
-    )
-    grad_query = jnp.einsum(
-        "bkgqj,bjkd->bqkgd", grad_scores, key_blocks, preferred_element_type=jnp.float32
-    )
-    grad_query = grad_query.astype(jnp.bfloat16).reshape(tok_rows, -1)
-    key_part = jnp.einsum(
-        "bkgqj,bqkgd->bjkd", grad_scores, query_blocks, preferred_element_type=jnp.float32
-    )
-    value_part = jnp.einsum(
-        "bkgqj,bqkgd->bjkd", probs_low, grad_out, preferred_element_type=jnp.float32
-    )
-    grad_parts = jnp.concatenate(
-        [
-            key_part.reshape(per_dev * nearby, BLOCK, kv_cols),
-            value_part.reshape(per_dev * nearby, BLOCK, kv_cols),
-        ],
-        axis=-1,
-    )
-    owed_grads = (
-        jnp.zeros((span_blocks, BLOCK, 2 * kv_cols), jnp.float32)
-        .at[local_index.reshape(-1)]
-        .add(grad_parts)
-    )
-    side = jnp.stack([owed_grads[:per_dev], owed_grads[2 * per_dev :]])
-    side = side.astype(jnp.bfloat16).reshape(2, TOK, KV)
-    mid = owed_grads[per_dev : 2 * per_dev].reshape(TOK, KV)
+    attended, grad_query, side, mid = attend(pattern, counts, query, cotangent, source)
     input_grad = scatter(grad_query, side, mid, full_wide)
-    return (attended.reshape(tok_rows, -1), input_grad)
+    return attended, input_grad
 
 
 def solution(mesh):

time: 256 us -> 223 us (0.87)
  matrix products: 21.5 us -> 0 us
  local copies, waits for them, and re-layouts: 27.7 us -> 7.2 us
  Pallas kernels: 193 us -> 212 us
  other arithmetic: 10.1 us -> 0 us
    dot_general x6 -> x0, matrix products: 21.5 us -> none  [the longest x1 6.4 us: body(): jnp.einsum('bqkgd,bjkd->bkgqj', grad_out, value_blocks, preferred_element...]
    pallas_call x0 -> x1, Pallas kernels: none -> 19.1 us  [attend(): pl.pallas_call(attend_kernel, name='attend', grid=(per_dev,), out_shape=(...]
    another operation x1 -> x0, local copies, waits for them, and re-layouts: 7.94 us -> none
    scatter-add x1 -> x0, other arithmetic: 3.73 us -> none  [body(): owed_grads = jnp.zeros((span_blocks, BLOCK, 2 * kv_cols), jnp.float32).at...]
    gather x4 -> x0, local copies, waits for them, and re-layouts: 3.43 us -> none  [the longest x2 2.04 us: body(): jnp.take(stacked, local_index, axis=0)]
    unnamed x16 -> x17, local copies, waits for them, and re-layouts: 9.86 us -> 7.2 us
where the time goes in v3:
time: 223 us; the launch traced here: 220 us
  Pallas kernels  212 us (95%)
  local copies, waits for them, and re-layouts  7.2 us (3%)
    pallas_call x1, Pallas kernels, gather(): pl.pallas_call(gather_kernel, name='gather_project', out_shape=(jax.Shape...  106 us
    pallas_call x1, Pallas kernels, scatter(): pl.pallas_call(scatter_kernel, name='project_scatter', out_shape=jax.Shap...  87 us
    pallas_call x1, Pallas kernels, attend(): pl.pallas_call(attend_kernel, name='attend', grid=(per_dev,), out_shape=(...  19.1 us
    unnamed x17, local copies, waits for them, and re-layouts  7.2 us

profile of v3, /device:TPU:10, one launch (start us, length us, event | category | flops | bytes accessed | tf_op | source)
XLA Modules:
  0.0 220.4 jit_solution(9680158365904837617)
XLA Ops:
  0.6 0.0 copy-start
  0.6 0.0 copy-start.3
  0.7 0.0 copy-start.4
  0.7 106.4 %gather_project.1 = (bf16[512,1024]{1,0:T(8,128)(2,1)}, bf16[3,512,256]{2,1,0:T(8,128)(2,1)}, bf16[8,1024,1280]{2,1,0:T(8,128)(2,1)}) custom-call(bf16[512,1024]{1,0:T(8,128)(2,1)} %x_in.1, bf16[512,1024]{1,0:T(8,128)(2,1)} %wq_in.1, bf16[512,128]{1,0:T(8,128)(2,1)} %wk_in.1, bf16[512,128]{1,0:T(8,128)(2,1)} %wv_in.1), custom_call_target="tpu_custom_call" | custom-call | flops 10737418240 | bytes 41943040 | tf_op jit(solution)/shard_map/gather_project/pallas_call | solution.py:255
  107.1 0.0 copy-done
  107.1 0.0 copy-done.3
  107.1 0.0 copy-done.4
  107.1 0.0 copy-start.1
  107.1 1.2 copy-done.1
  108.3 0.0 copy-start.2
  108.3 1.1 copy-done.2
  109.5 19.1 %attend.1 = (bf16[512,1024]{1,0:T(8,128)(2,1)}, bf16[512,1024]{1,0:T(8,128)(2,1)S(1)}, bf16[2,512,256]{2,1,0:T(8,128)(2,1)S(1)}, f32[512,256]{1,0:T(8,128)S(1)}) custom-call(s32[4,4]{1,0:T(4,128)S(1)} %copy-done.3, s32[64]{0:T(128)S(1)} %copy-done.4, bf16[512,1024]{1,0:T(8,128)(2,1)S(1)} %copy-done.1, bf16[512,1024]{1,0:T(8,128)(2,1)S(1)} %copy-done, ...), custom_call_target="tpu_custom_call" | custom-call | tf_op jit(solution)/shard_map/attend/pallas_call | solution.py:572
  128.6 0.0 copy-start.5
  128.6 1.0 copy-done.5
  129.5 0.0 copy-start.6
  129.5 0.8 copy-done.6
  130.4 0.0 copy-start.7
  130.4 0.8 copy-done.7
  131.1 87.0 %project_scatter.1 = bf16[512,1024]{1,0:T(8,128)(2,1)} custom-call(bf16[512,1024]{1,0:T(8,128)(2,1)} %copy-done.5, bf16[2,512,256]{2,1,0:T(8,128)(2,1)} %copy-done.6, f32[512,256]{1,0:T(8,128)} %copy-done.7, bf16[8,1024,1280]{2,1,0:T(8,128)(2,1)} %get-tuple-element.15.w_in), custom_call_target="tpu_custom_call" | custom-call | flops 10737418240 | bytes 25165824 | tf_op jit(solution)/shard_map/project_scatter/pallas_call | solution.py:459
  218.1 2.3 %copy.10 = bf16[512,1024]{1,0:T(8,128)(2,1)} copy(bf16[512,1024]{1,0:T(8,128)(2,1)} %project_scatter.1) | data formatting | bytes 2097152
Async XLA Ops:
  0.6 106.4 %copy-start = (bf16[512,1024]{1,0:T(8,128)(2,1)S(1)}, bf16[512,1024]{1,0:T(8,128)(2,1)}, u32[]{:S(2)}) copy-start(bf16[512,1024]{1,0:T(8,128)(2,1)} %cot_in.1) | copy-start | bytes 3145732
  0.6 106.4 %copy-start.3 = (s32[4,4]{1,0:T(4,128)S(1)}, s32[4,4]{1,0:T(4,128)}, u32[]{:S(2)}) copy-start(s32[4,4]{1,0:T(4,128)} %pattern.1) | copy-start | bytes 196
  0.7 106.4 %copy-start.4 = (s32[64]{0:T(128)S(1)}, s32[64]{0:T(128)}, u32[]{:S(2)}) copy-start(s32[64]{0:T(128)} %counts.1) | copy-start | bytes 772
  107.1 1.2 copy-start.1
  108.3 1.1 copy-start.2
  128.6 1.0 copy-start.5
  129.5 0.8 copy-start.6
  130.4 0.8 copy-start.7

commit v4 on v3

v4 whole, which is shorter than its diff:
```python
import functools

import jax
import jax.numpy as jnp
from jax import lax
from jax.experimental import pallas as pl
from jax.experimental.pallas import tpu as pltpu
from jax.sharding import PartitionSpec as P

HEADS = 64
KV_HEADS = 8
HEAD_DIM = 128
BLOCK = 128
GROUP = HEADS // KV_HEADS
ROWS = 16
COLS = 8
TOK = 512
HALF = 256
FEAT = 1024
KV = 256
WIDE = FEAT + KV
MESH = pl.DeviceIdType.MESH
MIB = 1024 * 1024


def place():
    row, col = lax.axis_index("row"), lax.axis_index("col")
    return row, col, row // 4, (row // 2) % 2, row % 2, col // 2, col % 2


def remote(src, dst, send, recv, row, col):
    return pltpu.make_async_remote_copy(
        src_ref=src,
        dst_ref=dst,
        send_sem=send,
        recv_sem=recv,
        device_id=(row, col),
        device_id_type=MESH,
    )


FAR = 64
NEAR_KINDS = {
    0: (1, 0, 0, HALF), 1: (1, 0, HALF, HALF), 2: (3, 0, HALF, HALF), 3: (3, 0, 0, HALF),
    4: (1, 3, 0, HALF), 5: (3, 1, HALF, HALF),
}
FEW_KINDS = {
    **NEAR_KINDS, 4: (1, 3, 0, FAR), 5: (3, 1, FAR, FAR), 6: (1, 0, 0, TOK), 7: (3, 0, 0, TOK),
}
ALL_COLS, Q_COLS, KV_COLS = (0, WIDE), (0, FEAT), (FEAT, KV)


def w_cols(plane, kind):
    return ALL_COLS if plane == 0 else KV_COLS if kind > 5 else Q_COLS


X_KINDS = (NEAR_KINDS, NEAR_KINDS)
W_KINDS = (NEAR_KINDS, FEW_KINDS)


def gather_kernel(
    x_in, wq_in, wk_in, wv_in,
    q_out, kv_out, w_out,
    xf, wf, acc, kv_buf,
    load_sem, send_sems, recv_sems, out_sem, kv_sem,
):
    row, col, y, h, k, z, l = place()
    prev_row, next_row = (row + ROWS - 1) % ROWS, (row + 1) % ROWS

    def row_of(yy, hh, kk):
        return (yy * 2 + hh) * 2 + kk

    y_to = {1: (row_of((y + 1) % 4, h, k), col), 3: (row_of((y + 3) % 4, h, k), col)}
    z_to = {1: (row, ((z + 1) % 4) * 2 + l), 3: (row, ((z + 3) % 4) * 2 + l)}
    h_pair, sibling = (row_of(y, 1 - h, k), col), (row_of(y, h, 1 - k), col)
    l_pair = (row, z * 2 + 1 - l)

    own_x, own_w = col, row // 2
    own_rows = pl.ds(k * TOK, TOK)
    loads = [
        pltpu.make_async_copy(x_in, xf.at[own_x], load_sem.at[0]),
        pltpu.make_async_copy(wq_in, wf.at[own_w, own_rows, pl.ds(0, FEAT)], load_sem.at[1]),
        pltpu.make_async_copy(wk_in, wf.at[own_w, own_rows, pl.ds(FEAT, 128)], load_sem.at[2]),
        pltpu.make_async_copy(
            wv_in, wf.at[own_w, own_rows, pl.ds(FEAT + 128, 128)], load_sem.at[3]
        ),
    ]
    for load in loads:
        load.start()

    barrier = pltpu.get_barrier_semaphore()
    peers = [
        z_to[1], z_to[3], l_pair, y_to[1], y_to[3], h_pair, sibling,
        (prev_row, col), (next_row, col),
    ]
    for peer in peers:
        pl.semaphore_signal(barrier, inc=1, device_id=peer, device_id_type=MESH)
    pl.semaphore_wait(barrier, len(peers))
    for load in loads:
        load.wait()

    index, started = {}, []

    def move(name, src, dst, peer):
        i = index.setdefault(name, len(index))
        return remote(src, dst, send_sems.at[i], recv_sems.at[i], *peer)

    def send(name, ref, peer):
        copy = move(name, ref, ref, peer)
        copy.start()
        started.append(copy)

    def got(name, ref):
        move(name, ref, ref, sibling).wait_recv()

    def x_part(step, plane, first, count):
        slot = ((z + step) % 4) * 2 + (l + plane) % 2
        return xf.at[slot, pl.ds(first, count)]

    def w_part(step, plane, first, count, cols=ALL_COLS, core=None):
        slot = ((y + step) % 4) * 2 + (h + plane) % 2
        core = k if core is None else core
        return wf.at[slot, pl.ds(core * TOK + first, count), pl.ds(*cols)]

    shared = []

    def share(step, plane, first, count, cols=ALL_COLS):
        part = (step, plane, first, count, cols)
        send(("s", *part), w_part(*part), sibling)
        shared.append(part)

    def take_shared():
        for part in shared:
            got(("s", *part), w_part(*part, 1 - k))
        shared.clear()

    def x_ring(plane, *kinds):
        for kind in kinds:
            way, step, first, count = X_KINDS[plane][kind]
            send(("x", plane, kind), x_part(step, plane, first, count), z_to[way])

    def x_got(plane, *kinds):
        for kind in kinds:
            way, step, first, count = X_KINDS[plane][kind]
            got(("x", plane, kind), x_part((step - way) % 4, plane, first, count))

    def w_ring(plane, *kinds):
        for kind in kinds:
            way, step, first, count = W_KINDS[plane][kind]
            part = (step, plane, first, count, w_cols(plane, kind))
            send(("w", plane, kind), w_part(*part), y_to[way])

    def w_got(plane, kind, *then):
        way, step, first, count = W_KINDS[plane][kind]
        part = ((step - way) % 4, plane, first, count, w_cols(plane, kind))
        got(("w", plane, kind), w_part(*part))
        w_ring(plane, *then)
        share(*part)

    def w_lend(name, step, first, count, cols):
        send((name, first, cols), w_part(step, 0, first, count, cols), h_pair)

    def w_lent(name, step, first, count, cols, *then):
        part = (step, 1, first, count, cols)
        got((name, first, cols), w_part(*part))
        w_ring(1, *then)
        share(*part)

    for kind in (0, 2, 1, 3):
        x_ring(0, kind)
        w_ring(0, kind)
    for half in range(2):
        send(("xp", half), x_part(0, 0, half * HALF, HALF), l_pair)
        share(0, 0, half * HALF, HALF)

    x_got(0, 0)
    x_ring(0, 4)
    x_got(0, 2)
    x_ring(0, 5)
    got(("xp", 0), x_part(0, 1, 0, HALF))
    x_ring(1, 0, 3)
    w_got(0, 0, 4)
    w_got(0, 2, 5)
    got(("xp", 1), x_part(0, 1, HALF, HALF))
    x_ring(1, 2, 1)
    w_lend("wp", 0, 0, TOK, KV_COLS)
    w_lend("wp", 0, 0, HALF, Q_COLS)
    x_got(0, 1, 3)
    w_got(0, 1)
    w_got(0, 3)
    w_lent("wp", 0, 0, TOK, KV_COLS, 6, 7)
    x_got(0, 4, 5)
    w_lent("wp", 0, 0, HALF, Q_COLS, 0, 3)
    w_lend("wp", 0, HALF, HALF, Q_COLS)
    w_got(0, 4)
    w_got(0, 5)
    x_got(1, 0)
    x_ring(1, 4)
    w_lent("wp", 0, HALF, HALF, Q_COLS, 1, 2)
    w_lend("wf", 2, 0, TOK, KV_COLS)
    w_lend("wf", 2, 2 * FAR, HALF - 2 * FAR, Q_COLS)
    w_lend("wf", 2, HALF, HALF, Q_COLS)
    x_got(1, 2)
    x_ring(1, 5)
    w_got(1, 6)
    w_got(1, 7)
    x_got(1, 1, 3)
    take_shared()

    late_x = ((z + 2) % 4) * 2 + 1 - l
    late_w = ((y + 2) % 4) * 2 + 1 - h

    def multiply(slot, tile):
        cols = pl.ds(pl.multiple_of(tile * 256, 256), 256)
        return jnp.dot(xf[slot], wf[slot, :, cols], preferred_element_type=jnp.float32)

    tiles = FEAT // 256

    @pl.loop(0, tiles)
    def _(tile):
        acc[tile] = jnp.zeros((TOK, 256), jnp.float32)

    def add_slots(wanted):
        @pl.loop(0, COLS)
        def _(slot):
            @pl.when(wanted(slot))
            def _():
                @pl.loop(0, tiles)
                def _(tile):
                    acc[tile] += multiply(slot, tile)

                pltpu.make_async_copy(wf.at[slot], w_out.at[slot], out_sem.at[slot]).start()

    def early(slot):
        here = (slot % 2 == h) | (slot // 2 == y)
        return here & (slot != late_x)

    add_slots(early)

    w_got(1, 0, 4)
    w_got(1, 3, 5)
    w_lent("wf", 2, 0, TOK, KV_COLS)
    x_got(1, 4, 5)
    take_shared()

    acc[tiles] = jnp.zeros((TOK, 256), jnp.float32)

    @pl.loop(0, COLS)
    def _(slot):
        acc[tiles] += multiply(slot, tiles)

    kv_buf[...] = acc[tiles].astype(jnp.bfloat16)
    halo = [
        move("up", kv_buf, kv_out.at[0], (next_row, col)),
        move("down", kv_buf, kv_out.at[2], (prev_row, col)),
    ]
    for copy in halo:
        copy.start()
    own_kv = pltpu.make_async_copy(kv_buf, kv_out.at[1], kv_sem)
    own_kv.start()

    w_lent("wf", 2, 2 * FAR, HALF - 2 * FAR, Q_COLS)
    w_got(1, 1)
    w_got(1, 2)
    take_shared()
    add_slots(lambda slot: jnp.logical_not(early(slot)) & (slot != late_w))
    w_lent("wf", 2, HALF, HALF, Q_COLS)
    w_got(1, 4)
    w_got(1, 5)
    take_shared()
    pltpu.make_async_copy(wf.at[late_w], w_out.at[late_w], out_sem.at[late_w]).start()

    @pl.loop(0, tiles)
    def _(tile):
        cols = pl.ds(pl.multiple_of(tile * 256, 256), 256)
        q_out[:, cols] = (acc[tile] + multiply(late_w, tile)).astype(jnp.bfloat16)

    for copy in started:
        copy.wait_send()
    for copy in halo:
        copy.wait()
    own_kv.wait()
    for slot in range(COLS):
        pltpu.make_async_copy(wf.at[slot], w_out.at[slot], out_sem.at[slot]).wait()
    assert len(index) <= SEMS


SEMS = 60


def gather(layer_input, w_query, w_key, w_value):
    dma = pltpu.SemaphoreType.DMA
    return pl.pallas_call(
        gather_kernel,
        name="gather_project",
        out_shape=(
            jax.ShapeDtypeStruct((TOK, FEAT), jnp.bfloat16),
            jax.ShapeDtypeStruct((3, TOK, KV), jnp.bfloat16),
            jax.ShapeDtypeStruct((COLS, FEAT, WIDE), jnp.bfloat16),
        ),
        in_specs=[pl.BlockSpec(memory_space=pl.ANY)] * 4,
        out_specs=(
            pl.BlockSpec(memory_space=pltpu.VMEM),
            pl.BlockSpec(memory_space=pl.ANY),
            pl.BlockSpec(memory_space=pl.ANY),
        ),
        scratch_shapes=[
            pltpu.VMEM((COLS, TOK, FEAT), jnp.bfloat16),
            pltpu.VMEM((COLS, FEAT, WIDE), jnp.bfloat16),
            pltpu.VMEM((WIDE // 256, TOK, 256), jnp.float32),
            pltpu.VMEM((TOK, KV), jnp.bfloat16),
            dma((4,)),
            dma((SEMS,)), dma((SEMS,)),
            dma((COLS,)), dma,
        ],
        compiler_params=pltpu.CompilerParams(
            collective_id=0, has_side_effects=True, vmem_limit_bytes=56 * MIB
        ),
        cost_estimate=pl.CostEstimate(
            flops=2 * TOK * 8192 * WIDE, bytes_accessed=40 * MIB, transcendentals=0
        ),
    )(layer_input, w_query, w_key, w_value)


def scatter_kernel(
    dq_in, side_in, mid_in, w_in,
    out,
    jn, wv, acc, pb, lent, far, near, pair_out, pair_in, side_got,
    w_sem, send_sems, recv_sems,
):
    row, col, y, h, k, z, l = place()
    prev_row, next_row = (row + ROWS - 1) % ROWS, (row + 1) % ROWS
    z_next, z_prev = (row, ((z + 1) % 4) * 2 + l), (row, ((z + 3) % 4) * 2 + l)
    l_pair = (row, z * 2 + 1 - l)

    def slot_of(step, plane):
        return ((z + step) % 4) * 2 + (l + plane) % 2

    order = [(2, 1), (1, 1), (3, 1), (2, 0), (1, 0), (3, 0), (0, 1), (0, 0)]
    loads = {}
    for i, (step, plane) in enumerate(order):
        slot = slot_of(step, plane)
        loads[step, plane] = pltpu.make_async_copy(w_in.at[slot], wv.at[slot], w_sem.at[i])
        loads[step, plane].start()

    barrier = pltpu.get_barrier_semaphore()
    peers = [z_next, z_prev, l_pair, (prev_row, col), (next_row, col)]
    for peer in peers:
        pl.semaphore_signal(barrier, inc=1, device_id=peer, device_id_type=MESH)
    jn[:, :FEAT] = dq_in[...]
    pl.semaphore_wait(barrier, len(peers))

    index, started = {}, []

    def send(name, src, dst, peer):
        i = index.setdefault(name, len(index))
        copy = remote(src, dst, send_sems.at[i], recv_sems.at[i], *peer)
        copy.start()
        started.append(copy)

    def got(name, ref):
        i = index[name]
        remote(ref, ref, send_sems.at[i], recv_sems.at[i], *l_pair).wait_recv()

    send("down", side_in.at[0], side_got.at[1], (prev_row, col))
    send("up", side_in.at[1], side_got.at[0], (next_row, col))

    tiles = FEAT // 256
    low, high, both = pl.ds(0, HALF), pl.ds(HALF, HALF), pl.ds(0, TOK)
    halves = (low, high)

    def product(slot, tile, rows, cols):
        tall = pl.ds(pl.multiple_of(tile * 256, 256), 256)
        return lax.dot_general(
            jn[rows, cols], wv[slot, tall, cols], (((1,), (1,)), ((), ())),
            preferred_element_type=jnp.float32,
        )

    def each_tile(step):
        @pl.loop(0, tiles)
        def _(tile):
            step(tile, pl.ds(pl.multiple_of(tile * 256, 256), 256))

    every = pl.ds(0, WIDE)

    def fill(target, step, plane, rows, extra=None):
        slot = slot_of(step, plane)

        def one(tile, cols):
            value = product(slot, tile, rows, every)
            if extra is not None:
                value += extra[:, cols].astype(jnp.float32)
            target[rows, cols] = value.astype(jnp.bfloat16)

        each_tile(one)

    first = [(2, 1), (1, 1), (3, 1)]
    for i, (step, plane) in enumerate(first):
        loads[step, plane].wait()
        slot = slot_of(step, plane)

        def query_part(tile, cols):
            acc[i, tile] = product(slot, tile, both, pl.ds(0, FEAT))

        each_tile(query_part)

    got("down", side_got.at[1])
    got("up", side_got.at[0])
    jn[:, FEAT:] = (
        mid_in[...] + side_got[0].astype(jnp.float32) + side_got[1].astype(jnp.float32)
    ).astype(jnp.bfloat16)

    for half, rows in enumerate(halves):
        for i, (step, plane) in enumerate(first):
            slot = slot_of(step, plane)

            def whole(tile, cols):
                value = acc[i, tile, rows] + product(slot, tile, rows, pl.ds(FEAT, KV))
                pb[1, i, rows, cols] = value.astype(jnp.bfloat16)

            each_tile(whole)
            source = pb.at[1, i, rows]
            if i == 0:
                send(("lend", half), source, lent.at[rows], l_pair)
            else:
                target = near.at[1, i - 1, rows]
                send(("near", 1, i - 1, half), source, target, z_next if i == 1 else z_prev)

    def near_half(way, half, extra=None):
        rows = halves[half]
        fill(pb.at[0, 1 + way], 1 if way == 0 else 3, 0, rows, extra)
        send(
            ("near", 0, way, half), pb.at[0, 1 + way, rows], near.at[0, way, rows],
            z_next if way == 0 else z_prev,
        )

    loads[2, 0].wait()
    for half, rows in enumerate(halves):
        got(("lend", half), lent.at[rows])
        fill(pb.at[0, 0], 2, 0, rows, lent.at[rows])
        send(("far", half), pb.at[0, 0, rows], far.at[half], z_prev if half else z_next)
    loads[1, 0].wait()
    loads[3, 0].wait()
    near_half(0, 1)
    near_half(1, 0)

    def own(plane):
        loads[0, plane].wait()

        def one(tile, cols):
            acc[plane, tile] = product(slot_of(0, plane), tile, both, every)

        each_tile(one)

    def add_near(plane, way, half):
        rows = halves[half]
        got(("near", plane, way, half), near.at[plane, way, rows])

        def one(tile, cols):
            acc[plane, tile, rows] += near[plane, way, rows, cols].astype(jnp.float32)

        each_tile(one)

    own(1)
    for half, rows in enumerate(halves):
        for way in range(2):
            got(("near", 1, way, half), near.at[1, way, rows])

        def pair_sum(tile, cols):
            value = acc[1, tile, rows] + near[1, 0, rows, cols].astype(jnp.float32)
            value += near[1, 1, rows, cols].astype(jnp.float32)
            pair_out[rows, cols] = value.astype(jnp.bfloat16)

        each_tile(pair_sum)
        send(("pair", half), pair_out.at[rows], pair_in.at[rows], l_pair)
    got(("far", 0), far.at[0])
    near_half(0, 0, far.at[0])
    got(("far", 1), far.at[1])
    near_half(1, 1, far.at[1])
    own(0)
    add_near(0, 0, 1)
    add_near(0, 1, 0)
    for half, rows in enumerate(halves):
        got(("pair", half), pair_in.at[rows])

        def add_pair(tile, cols):
            acc[0, tile, rows] += pair_in[rows, cols].astype(jnp.float32)

        each_tile(add_pair)
    for half, rows in enumerate(halves):
        got(("near", 0, half, half), near.at[0, half, rows])

        def last(tile, cols):
            value = acc[0, tile, rows] + near[0, half, rows, cols].astype(jnp.float32)
            out[rows, cols] = value.astype(jnp.bfloat16)

        each_tile(last)

    for copy in started:
        copy.wait_send()


def scatter(grad_query, side, mid, full_wide):
    dma = pltpu.SemaphoreType.DMA
    vmem = pl.BlockSpec(memory_space=pltpu.VMEM)
    low = jnp.bfloat16
    return pl.pallas_call(
        scatter_kernel,
        name="project_scatter",
        out_shape=jax.ShapeDtypeStruct((TOK, FEAT), low),
        in_specs=[vmem, vmem, vmem, pl.BlockSpec(memory_space=pl.ANY)],
        out_specs=vmem,
        scratch_shapes=[
            pltpu.VMEM((TOK, WIDE), low),
            pltpu.VMEM((COLS, FEAT, WIDE), low),
            pltpu.VMEM((3, FEAT // 256, TOK, 256), jnp.float32),
            pltpu.VMEM((2, 3, TOK, FEAT), low),
            pltpu.VMEM((TOK, FEAT), low),
            pltpu.VMEM((2, HALF, FEAT), low),
            pltpu.VMEM((2, 2, TOK, FEAT), low),
            pltpu.VMEM((TOK, FEAT), low),
            pltpu.VMEM((TOK, FEAT), low),
            pltpu.VMEM((2, TOK, KV), low),
            dma((COLS,)),
            dma((16,)), dma((16,)),
        ],
        compiler_params=pltpu.CompilerParams(
            collective_id=1, has_side_effects=True, vmem_limit_bytes=56 * MIB
        ),
        cost_estimate=pl.CostEstimate(
            flops=2 * TOK * 8192 * WIDE, bytes_accessed=24 * MIB, transcendentals=0
        ),
    )(grad_query, side, mid, full_wide)


def attend_kernel(
    pattern, counts, q_in, cot_in, kv_in,
    out, dq_out, side_out, mid_out,
    owed,
):
    block = pl.program_id(0)
    per_dev = TOK // BLOCK
    block_count = ROWS * per_dev
    first = lax.axis_index("row") * per_dev
    scale = HEAD_DIM ** (-0.5)
    pair = 2 * HEAD_DIM

    @pl.when(block == 0)
    def _():
        owed[...] = jnp.zeros_like(owed)

    chosen = [pattern[block, i] for i in range(4)]
    local = [(b - first + per_dev + block_count) % block_count for b in chosen]
    keys = jnp.concatenate([kv_in[i, :, :HEAD_DIM] for i in local], axis=0)
    values = jnp.concatenate([kv_in[i, :, HEAD_DIM:] for i in local], axis=0)
    keys_t, values_t = keys.T, values.T
    spot = lax.broadcasted_iota(jnp.int32, (BLOCK, pair), 0)
    live = jnp.concatenate([spot < counts[b] for b in chosen], axis=0)
    own_count = counts[first + block]
    lane = lax.broadcasted_iota(jnp.int32, (HEAD_DIM, pair), 1)
    query_live = jnp.where(lane % BLOCK < own_count, 1.0, 0.0)
    row_live = lax.broadcasted_iota(jnp.int32, (BLOCK, HEAD_DIM), 0) < own_count
    row_live = jnp.where(row_live, 1.0, 0.0).astype(jnp.bfloat16)

    def heads(ref, start, mask=None):
        parts = [ref[:, start + i * HEAD_DIM : start + (i + 1) * HEAD_DIM] for i in range(2)]
        if mask is not None:
            parts = [part * mask for part in parts]
        return jnp.concatenate(parts, axis=0)

    def dot(a, b, dims):
        return lax.dot_general(a, b, (dims, ((), ())), preferred_element_type=jnp.float32)

    def put(ref, start, both):
        low = both.astype(jnp.bfloat16)
        for i in range(2):
            cols = slice(start + i * HEAD_DIM, start + (i + 1) * HEAD_DIM)
            ref[:, cols] = low[:, i * HEAD_DIM : (i + 1) * HEAD_DIM].T

    grad_keys = grad_values = None
    for start in range(0, FEAT, pair):
        query = heads(q_in, start)
        grad_out = heads(cot_in, start, row_live)
        raw = jnp.where(live, dot(keys, query, ((1,), (1,))), -1e30)
        top = jnp.max(raw, axis=0, keepdims=True)
        power = jnp.exp((raw - top) * scale)
        probs = power * (1.0 / jnp.sum(power, axis=0, keepdims=True))
        probs_low = probs.astype(jnp.bfloat16)
        put(out, start, dot(values_t, probs_low, ((1,), (0,))) * query_live)
        grad_probs = dot(values, grad_out, ((1,), (1,)))
        delta = jnp.sum(probs_low.astype(jnp.float32) * grad_probs, axis=0, keepdims=True)
        grad_scores = (probs * (grad_probs - delta) * scale).astype(jnp.bfloat16)
        put(dq_out, start, dot(keys_t, grad_scores, ((1,), (0,))))
        key_part = dot(grad_scores, query, ((1,), (0,)))
        value_part = dot(probs_low, grad_out, ((1,), (0,)))
        grad_keys = key_part if grad_keys is None else grad_keys + key_part
        grad_values = value_part if grad_values is None else grad_values + value_part

    for i, spot in enumerate(local):
        rows = slice(i * BLOCK, (i + 1) * BLOCK)
        owed[spot, :, :HEAD_DIM] += grad_keys[rows]
        owed[spot, :, HEAD_DIM:] += grad_values[rows]

    @pl.when(block == per_dev - 1)
    def _():
        for i in range(per_dev):
            rows = slice(i * BLOCK, (i + 1) * BLOCK)
            side_out[0, rows] = owed[i].astype(jnp.bfloat16)
            mid_out[rows] = owed[per_dev + i]
            side_out[1, rows] = owed[2 * per_dev + i].astype(jnp.bfloat16)


def attend(pattern, counts, query, cotangent, source):
    per_dev = TOK // BLOCK
    tokens = pl.BlockSpec((BLOCK, FEAT), lambda b: (b, 0))
    smem = pl.BlockSpec(memory_space=pltpu.SMEM)
    low = jnp.bfloat16
    return pl.pallas_call(
        attend_kernel,
        name="attend",
        grid=(per_dev,),
        out_shape=(
            jax.ShapeDtypeStruct((TOK, FEAT), low),
            jax.ShapeDtypeStruct((TOK, FEAT), low),
            jax.ShapeDtypeStruct((2, TOK, KV), low),
            jax.ShapeDtypeStruct((TOK, KV), jnp.float32),
        ),
        in_specs=[
            smem, smem, tokens, tokens,
            pl.BlockSpec((3 * per_dev, BLOCK, KV), lambda b: (0, 0, 0)),
        ],
        out_specs=(
            tokens, tokens,
            pl.BlockSpec((2, TOK, KV), lambda b: (0, 0, 0)),
            pl.BlockSpec((TOK, KV), lambda b: (0, 0)),
        ),
        scratch_shapes=[pltpu.VMEM((3 * per_dev, BLOCK, KV), jnp.float32)],
        compiler_params=pltpu.CompilerParams(vmem_limit_bytes=62 * MIB),
    )(pattern, counts, query, cotangent, source.reshape(3 * per_dev, BLOCK, KV))


def body(layer_input, w_query, w_key, w_value, counts, pattern, cotangent):
    query, source, full_wide = gather(layer_input, w_query, w_key, w_value)
    attended, grad_query, side, mid = attend(pattern, counts, query, cotangent, source)
    input_grad = scatter(grad_query, side, mid, full_wide)
    return attended, input_grad


def solution(mesh):
    placed = (
        P("row", "col"),
        P("row", "col"),
        P("row", "col"),
        P("row", "col"),
        P(),
        P("row", None),
        P("row", "col"),
    )
    return jax.shard_map(
        body,
        mesh=mesh,
        in_specs=placed,
        out_specs=(P("row", "col"), P("row", "col")),
        check_vma=False,
    )
```

time: 223 us -> 193 us (0.87)
  Pallas kernels: 212 us -> 189 us
  local copies, waits for them, and re-layouts: 7.2 us -> 2.26 us
    pallas_call x1, Pallas kernels: 106 us -> 93.3 us  [gather(): pl.pallas_call(gather_kernel, name='gather_project', out_shape=(jax.Shape...]
    pallas_call x1, Pallas kernels: 87 us -> 75.7 us  [scatter(): pl.pallas_call(scatter_kernel, name='project_scatter', out_shape=jax.Shap...]
    unnamed x17 -> x1, local copies, waits for them, and re-layouts: 7.2 us -> 2.26 us
where the time goes in v4:
time: 193 us; the launch traced here: 192 us
  Pallas kernels  189 us (98%)
  local copies, waits for them, and re-layouts  2.26 us (1%)
    pallas_call x1, Pallas kernels, gather(): pl.pallas_call(gather_kernel, name='gather_project', out_shape=(jax.Shape...  93.3 us
    pallas_call x1, Pallas kernels, scatter(): pl.pallas_call(scatter_kernel, name='project_scatter', out_shape=jax.Shap...  75.7 us
    pallas_call x1, Pallas kernels, attend(): pl.pallas_call(attend_kernel, name='attend', grid=(per_dev,), out_shape=(...  20.4 us

profile of v4, /device:TPU:10, one launch (start us, length us, event | category | flops | bytes accessed | tf_op | source)
XLA Modules:
  0.0 192.3 jit_solution(15174185544494016715)
XLA Ops:
  0.6 93.3 %gather_project.1 = (bf16[512,1024]{1,0:T(8,128)(2,1)}, bf16[3,512,256]{2,1,0:T(8,128)(2,1)}, bf16[8,1024,1280]{2,1,0:T(8,128)(2,1)}) custom-call(bf16[512,1024]{1,0:T(8,128)(2,1)} %x_in.1, bf16[512,1024]{1,0:T(8,128)(2,1)} %wq_in.1, bf16[512,128]{1,0:T(8,128)(2,1)} %wk_in.1, bf16[512,128]{1,0:T(8,128)(2,1)} %wv_in.1), custom_call_target="tpu_custom_call" | custom-call | flops 10737418240 | bytes 41943040 | tf_op jit(solution)/shard_map/gather_project/pallas_call | solution.py:293
  93.9 20.4 %attend.1 = (bf16[512,1024]{1,0:T(8,128)(2,1)}, bf16[512,1024]{1,0:T(8,128)(2,1)}, bf16[2,512,256]{2,1,0:T(8,128)(2,1)}, f32[512,256]{1,0:T(8,128)}) custom-call(s32[4,4]{1,0:T(4,128)} %pattern.1, s32[64]{0:T(128)} %counts.1, bf16[512,1024]{1,0:T(8,128)(2,1)} %get-tuple-element.9.q_in, bf16[512,1024]{1,0:T(8,128)(2,1)} %cot_in.1, bf16[12,128,256]{2,1,0:T(8,128)(2,1)} %bitcast.1), custom_call_target="tpu_custom_call" | custom-call | tf_op jit(solution)/shard_map/attend/pallas_call | solution.py:618
  114.3 75.7 %project_scatter.1 = bf16[512,1024]{1,0:T(8,128)(2,1)} custom-call(bf16[512,1024]{1,0:T(8,128)(2,1)} %get-tuple-element.12.dq_in, bf16[2,512,256]{2,1,0:T(8,128)(2,1)} %get-tuple-element.13.side_in, f32[512,256]{1,0:T(8,128)} %get-tuple-element.14.mid_in, bf16[8,1024,1280]{2,1,0:T(8,128)(2,1)} %get-tuple-element.15.w_in), custom_call_target="tpu_custom_call" | custom-call | flops 10737418240 | bytes 25165824 | tf_op jit(solution)/shard_map/project_scatter/pallas_call | solution.py:507
  190.1 2.3 %copy.10 = bf16[512,1024]{1,0:T(8,128)(2,1)} copy(bf16[512,1024]{1,0:T(8,128)(2,1)} %project_scatter.1) | data formatting | bytes 2097152

commit v5 on v4

--- a/solution.py
+++ b/solution.py
@@ -21,6 +21,7 @@
 WIDE = FEAT + KV
 MESH = pl.DeviceIdType.MESH
 MIB = 1024 * 1024
+LOG2E = 1.4426950408889634
 
 
 def place():
@@ -39,7 +40,7 @@
     )
 
 
-FAR = 64
+FAR = 96
 NEAR_KINDS = {
     0: (1, 0, 0, HALF), 1: (1, 0, HALF, HALF), 2: (3, 0, HALF, HALF), 3: (3, 0, 0, HALF),
     4: (1, 3, 0, HALF), 5: (3, 1, HALF, HALF),
@@ -61,8 +62,8 @@
 def gather_kernel(
     x_in, wq_in, wk_in, wv_in,
     q_out, kv_out, w_out,
-    xf, wf, acc, kv_buf,
-    load_sem, send_sems, recv_sems, out_sem, kv_sem,
+    xf, wf, acc, kv_buf, q_buf,
+    load_sem, send_sems, recv_sems, out_sem, kv_sem, q_sem,
 ):
     row, col, y, h, k, z, l = place()
     prev_row, next_row = (row + ROWS - 1) % ROWS, (row + 1) % ROWS
@@ -273,13 +274,17 @@
     @pl.loop(0, tiles)
     def _(tile):
         cols = pl.ds(pl.multiple_of(tile * 256, 256), 256)
-        q_out[:, cols] = (acc[tile] + multiply(late_w, tile)).astype(jnp.bfloat16)
+        q_buf[:, cols] = (acc[tile] + multiply(late_w, tile)).astype(jnp.bfloat16)
+        pltpu.make_async_copy(q_buf.at[:, cols], q_out.at[:, cols], q_sem.at[tile]).start()
 
     for copy in started:
         copy.wait_send()
     for copy in halo:
         copy.wait()
     own_kv.wait()
+    for tile in range(tiles):
+        cols = pl.ds(tile * 256, 256)
+        pltpu.make_async_copy(q_buf.at[:, cols], q_out.at[:, cols], q_sem.at[tile]).wait()
     for slot in range(COLS):
         pltpu.make_async_copy(wf.at[slot], w_out.at[slot], out_sem.at[slot]).wait()
     assert len(index) <= SEMS
@@ -300,7 +305,7 @@
         ),
         in_specs=[pl.BlockSpec(memory_space=pl.ANY)] * 4,
         out_specs=(
-            pl.BlockSpec(memory_space=pltpu.VMEM),
+            pl.BlockSpec(memory_space=pl.ANY),
             pl.BlockSpec(memory_space=pl.ANY),
             pl.BlockSpec(memory_space=pl.ANY),
         ),
@@ -309,9 +314,10 @@
             pltpu.VMEM((COLS, FEAT, WIDE), jnp.bfloat16),
             pltpu.VMEM((WIDE // 256, TOK, 256), jnp.float32),
             pltpu.VMEM((TOK, KV), jnp.bfloat16),
+            pltpu.VMEM((TOK, FEAT), jnp.bfloat16),
             dma((4,)),
             dma((SEMS,)), dma((SEMS,)),
-            dma((COLS,)), dma,
+            dma((COLS,)), dma, dma((FEAT // 256,)),
         ],
         compiler_params=pltpu.CompilerParams(
             collective_id=0, has_side_effects=True, vmem_limit_bytes=56 * MIB
@@ -325,8 +331,8 @@
 def scatter_kernel(
     dq_in, side_in, mid_in, w_in,
     out,
-    jn, wv, acc, pb, lent, far, near, pair_out, pair_in, side_got,
-    w_sem, send_sems, recv_sems,
+    jn, wv, acc, pb, lent, far, near, pair_out, pair_in, side_got, mid, result,
+    w_sem, load_sem, out_sem, send_sems, recv_sems,
 ):
     row, col, y, h, k, z, l = place()
     prev_row, next_row = (row + ROWS - 1) % ROWS, (row + 1) % ROWS
@@ -337,17 +343,20 @@
         return ((z + step) % 4) * 2 + (l + plane) % 2
 
     order = [(2, 1), (1, 1), (3, 1), (2, 0), (1, 0), (3, 0), (0, 1), (0, 0)]
+    load_query = pltpu.make_async_copy(dq_in, jn.at[:, pl.ds(0, FEAT)], load_sem.at[0])
+    load_mid = pltpu.make_async_copy(mid_in, mid, load_sem.at[1])
+    load_query.start()
     loads = {}
     for i, (step, plane) in enumerate(order):
         slot = slot_of(step, plane)
         loads[step, plane] = pltpu.make_async_copy(w_in.at[slot], wv.at[slot], w_sem.at[i])
         loads[step, plane].start()
+    load_mid.start()
 
     barrier = pltpu.get_barrier_semaphore()
     peers = [z_next, z_prev, l_pair, (prev_row, col), (next_row, col)]
     for peer in peers:
         pl.semaphore_signal(barrier, inc=1, device_id=peer, device_id_type=MESH)
-    jn[:, :FEAT] = dq_in[...]
     pl.semaphore_wait(barrier, len(peers))
 
     index, started = {}, []
@@ -395,36 +404,46 @@
         each_tile(one)
 
     first = [(2, 1), (1, 1), (3, 1)]
+    load_query.wait()
     for i, (step, plane) in enumerate(first):
         loads[step, plane].wait()
-        slot = slot_of(step, plane)
-
-        def query_part(tile, cols):
-            acc[i, tile] = product(slot, tile, both, pl.ds(0, FEAT))
-
-        each_tile(query_part)
-
-    got("down", side_got.at[1])
-    got("up", side_got.at[0])
-    jn[:, FEAT:] = (
-        mid_in[...] + side_got[0].astype(jnp.float32) + side_got[1].astype(jnp.float32)
-    ).astype(jnp.bfloat16)
-
-    for half, rows in enumerate(halves):
+
+    def query_part(rows):
         for i, (step, plane) in enumerate(first):
             slot = slot_of(step, plane)
 
-            def whole(tile, cols):
+            def one(tile, cols):
+                acc[i, tile, rows] = product(slot, tile, rows, pl.ds(0, FEAT))
+
+            each_tile(one)
+
+    def whole_part(half):
+        rows = halves[half]
+        for i, (step, plane) in enumerate(first):
+            slot = slot_of(step, plane)
+
+            def one(tile, cols):
                 value = acc[i, tile, rows] + product(slot, tile, rows, pl.ds(FEAT, KV))
                 pb[1, i, rows, cols] = value.astype(jnp.bfloat16)
 
-            each_tile(whole)
+            each_tile(one)
             source = pb.at[1, i, rows]
             if i == 0:
                 send(("lend", half), source, lent.at[rows], l_pair)
             else:
                 target = near.at[1, i - 1, rows]
                 send(("near", 1, i - 1, half), source, target, z_next if i == 1 else z_prev)
+
+    query_part(low)
+    load_mid.wait()
+    got("down", side_got.at[1])
+    got("up", side_got.at[0])
+    jn[:, FEAT:] = (
+        mid[...] + side_got[0].astype(jnp.float32) + side_got[1].astype(jnp.float32)
+    ).astype(jnp.bfloat16)
+    whole_part(0)
+    query_part(high)
+    whole_part(1)
 
     def near_half(way, half, extra=None):
         rows = halves[half]
@@ -492,24 +511,27 @@
 
         def last(tile, cols):
             value = acc[0, tile, rows] + near[0, half, rows, cols].astype(jnp.float32)
-            out[rows, cols] = value.astype(jnp.bfloat16)
+            result[rows, cols] = value.astype(jnp.bfloat16)
 
         each_tile(last)
+        pltpu.make_async_copy(result.at[rows], out.at[rows], out_sem.at[half]).start()
 
     for copy in started:
         copy.wait_send()
+    for half, rows in enumerate(halves):
+        pltpu.make_async_copy(result.at[rows], out.at[rows], out_sem.at[half]).wait()
 
 
 def scatter(grad_query, side, mid, full_wide):
     dma = pltpu.SemaphoreType.DMA
-    vmem = pl.BlockSpec(memory_space=pltpu.VMEM)
+    anywhere = pl.BlockSpec(memory_space=pl.ANY)
     low = jnp.bfloat16
     return pl.pallas_call(
         scatter_kernel,
         name="project_scatter",
         out_shape=jax.ShapeDtypeStruct((TOK, FEAT), low),
-        in_specs=[vmem, vmem, vmem, pl.BlockSpec(memory_space=pl.ANY)],
-        out_specs=vmem,
+        in_specs=[anywhere] * 4,
+        out_specs=anywhere,
         scratch_shapes=[
             pltpu.VMEM((TOK, WIDE), low),
             pltpu.VMEM((COLS, FEAT, WIDE), low),
@@ -521,7 +543,9 @@
             pltpu.VMEM((TOK, FEAT), low),
             pltpu.VMEM((TOK, FEAT), low),
             pltpu.VMEM((2, TOK, KV), low),
-            dma((COLS,)),
+            pltpu.VMEM((TOK, KV), jnp.float32),
+            pltpu.VMEM((TOK, FEAT), low),
+            dma((COLS,)), dma((2,)), dma((2,)),
             dma((16,)), dma((16,)),
         ],
         compiler_params=pltpu.CompilerParams(
@@ -543,6 +567,7 @@
     block_count = ROWS * per_dev
     first = lax.axis_index("row") * per_dev
     scale = HEAD_DIM ** (-0.5)
+    exponent_scale = scale * LOG2E
     pair = 2 * HEAD_DIM
 
     @pl.when(block == 0)
@@ -557,7 +582,7 @@
     spot = lax.broadcasted_iota(jnp.int32, (BLOCK, pair), 0)
     live = jnp.concatenate([spot < counts[b] for b in chosen], axis=0)
     own_count = counts[first + block]
-    lane = lax.broadcasted_iota(jnp.int32, (HEAD_DIM, pair), 1)
+    lane = lax.broadcasted_iota(jnp.int32, (1, pair), 1)
     query_live = jnp.where(lane % BLOCK < own_count, 1.0, 0.0)
     row_live = lax.broadcasted_iota(jnp.int32, (BLOCK, HEAD_DIM), 0) < own_count
     row_live = jnp.where(row_live, 1.0, 0.0).astype(jnp.bfloat16)
@@ -577,24 +602,43 @@
             cols = slice(start + i * HEAD_DIM, start + (i + 1) * HEAD_DIM)
             ref[:, cols] = low[:, i * HEAD_DIM : (i + 1) * HEAD_DIM].T
 
-    grad_keys = grad_values = None
-    for start in range(0, FEAT, pair):
+    def begin(start):
         query = heads(q_in, start)
         grad_out = heads(cot_in, start, row_live)
-        raw = jnp.where(live, dot(keys, query, ((1,), (1,))), -1e30)
+        raw = dot(keys, query, ((1,), (1,)))
+        return start, query, grad_out, raw, dot(values, grad_out, ((1,), (1,)))
+
+    def middle(start, query, grad_out, raw, grad_probs):
+        raw = jnp.where(live, raw, -1e30)
         top = jnp.max(raw, axis=0, keepdims=True)
-        power = jnp.exp((raw - top) * scale)
+        power = jnp.exp2((raw - top) * exponent_scale)
         probs = power * (1.0 / jnp.sum(power, axis=0, keepdims=True))
         probs_low = probs.astype(jnp.bfloat16)
-        put(out, start, dot(values_t, probs_low, ((1,), (0,))) * query_live)
-        grad_probs = dot(values, grad_out, ((1,), (1,)))
         delta = jnp.sum(probs_low.astype(jnp.float32) * grad_probs, axis=0, keepdims=True)
         grad_scores = (probs * (grad_probs - delta) * scale).astype(jnp.bfloat16)
+        return start, query, grad_out, probs_low, grad_scores
+
+    def end(start, query, grad_out, probs_low, grad_scores):
+        put(out, start, dot(values_t, probs_low, ((1,), (0,))) * query_live)
         put(dq_out, start, dot(keys_t, grad_scores, ((1,), (0,))))
         key_part = dot(grad_scores, query, ((1,), (0,)))
         value_part = dot(probs_low, grad_out, ((1,), (0,)))
-        grad_keys = key_part if grad_keys is None else grad_keys + key_part
-        grad_values = value_part if grad_values is None else grad_values + value_part
+        return key_part, value_part
+
+    starts = range(0, FEAT, pair)
+    parts = []
+    coming, going = begin(starts[0]), None
+    for i in range(len(starts)):
+        now = coming
+        if i + 1 < len(starts):
+            coming = begin(starts[i + 1])
+        done = middle(*now)
+        if going is not None:
+            parts.append(end(*going))
+        going = done
+    parts.append(end(*going))
+    grad_keys = sum(part[0] for part in parts[1:]) + parts[0][0]
+    grad_values = sum(part[1] for part in parts[1:]) + parts[0][1]
 
     for i, spot in enumerate(local):
         rows = slice(i * BLOCK, (i + 1) * BLOCK)

time: 193 us -> 183 us (0.948)
  Pallas kernels: 189 us -> 179 us
    pallas_call x1, Pallas kernels: 20.4 us -> 11.7 us  [attend(): pl.pallas_call(attend_kernel, name='attend', grid=(per_dev,), out_shape=(...]
where the time goes in v5:
time: 183 us; the launch traced here: 182 us
  Pallas kernels  179 us (98%)
  local copies, waits for them, and re-layouts  2.26 us (1%)
    pallas_call x1, Pallas kernels, gather(): pl.pallas_call(gather_kernel, name='gather_project', out_shape=(jax.Shape...  93 us
    pallas_call x1, Pallas kernels, scatter(): pl.pallas_call(scatter_kernel, name='project_scatter', out_shape=jax.Shap...  74.3 us
    pallas_call x1, Pallas kernels, attend(): pl.pallas_call(attend_kernel, name='attend', grid=(per_dev,), out_shape=(...  11.7 us

profile of v5, /device:TPU:10, one launch (start us, length us, event | category | flops | bytes accessed | tf_op | source)
XLA Modules:
  0.0 181.9 jit_solution(9210252895068259612)
XLA Ops:
  0.6 93.0 %gather_project.1 = (bf16[512,1024]{1,0:T(8,128)(2,1)}, bf16[3,512,256]{2,1,0:T(8,128)(2,1)}, bf16[8,1024,1280]{2,1,0:T(8,128)(2,1)}) custom-call(bf16[512,1024]{1,0:T(8,128)(2,1)} %x_in.1, bf16[512,1024]{1,0:T(8,128)(2,1)} %wq_in.1, bf16[512,128]{1,0:T(8,128)(2,1)} %wk_in.1, bf16[512,128]{1,0:T(8,128)(2,1)} %wv_in.1), custom_call_target="tpu_custom_call" | custom-call | flops 10737418240 | bytes 41943040 | tf_op jit(solution)/shard_map/gather_project/pallas_call | solution.py:298
  93.6 11.7 %attend.1 = (bf16[512,1024]{1,0:T(8,128)(2,1)}, bf16[512,1024]{1,0:T(8,128)(2,1)}, bf16[2,512,256]{2,1,0:T(8,128)(2,1)}, f32[512,256]{1,0:T(8,128)}) custom-call(s32[4,4]{1,0:T(4,128)} %pattern.1, s32[64]{0:T(128)} %counts.1, bf16[512,1024]{1,0:T(8,128)(2,1)} %get-tuple-element.9.q_in, bf16[512,1024]{1,0:T(8,128)(2,1)} %cot_in.1, bf16[12,128,256]{2,1,0:T(8,128)(2,1)} %bitcast.1), custom_call_target="tpu_custom_call" | custom-call | tf_op jit(solution)/shard_map/attend/pallas_call | solution.py:662
  105.4 74.3 %project_scatter.1 = bf16[512,1024]{1,0:T(8,128)(2,1)} custom-call(bf16[512,1024]{1,0:T(8,128)(2,1)} %get-tuple-element.12.dq_in, bf16[2,512,256]{2,1,0:T(8,128)(2,1)} %get-tuple-element.13.side_in, f32[512,256]{1,0:T(8,128)} %get-tuple-element.14.mid_in, bf16[8,1024,1280]{2,1,0:T(8,128)(2,1)} %get-tuple-element.15.w_in), custom_call_target="tpu_custom_call" | custom-call | flops 10737418240 | bytes 25165824 | tf_op jit(solution)/shard_map/project_scatter/pallas_call | solution.py:529
  179.6 2.3 %copy.10 = bf16[512,1024]{1,0:T(8,128)(2,1)} copy(bf16[512,1024]{1,0:T(8,128)(2,1)} %project_scatter.1) | data formatting | bytes 2097152

commit v6 on v5

--- a/solution.py
+++ b/solution.py
@@ -20,6 +20,10 @@
 KV = 256
 WIDE = FEAT + KV
 MESH = pl.DeviceIdType.MESH
+SPAN = 1024
+LAST = 2
+LEND = 64
+OUT_SPAN = 1024
 MIB = 1024 * 1024
 LOG2E = 1.4426950408889634
 
@@ -62,7 +66,7 @@
 def gather_kernel(
     x_in, wq_in, wk_in, wv_in,
     q_out, kv_out, w_out,
-    xf, wf, acc, kv_buf, q_buf,
+    xf, wf, acc, kv_acc, kv_buf, q_buf,
     load_sem, send_sems, recv_sems, out_sem, kv_sem, q_sem,
 ):
     row, col, y, h, k, z, l = place()
@@ -211,15 +215,18 @@
     late_x = ((z + 2) % 4) * 2 + 1 - l
     late_w = ((y + 2) % 4) * 2 + 1 - h
 
-    def multiply(slot, tile):
-        cols = pl.ds(pl.multiple_of(tile * 256, 256), 256)
+    def multiply(slot, first, count):
+        cols = pl.ds(first, count)
         return jnp.dot(xf[slot], wf[slot, :, cols], preferred_element_type=jnp.float32)
 
-    tiles = FEAT // 256
+    def multiply_tile(slot, tile):
+        return multiply(slot, pl.multiple_of(tile * SPAN, SPAN), SPAN)
+
+    tiles = FEAT // SPAN
 
     @pl.loop(0, tiles)
     def _(tile):
-        acc[tile] = jnp.zeros((TOK, 256), jnp.float32)
+        acc[tile] = jnp.zeros((TOK, SPAN), jnp.float32)
 
     def add_slots(wanted):
         @pl.loop(0, COLS)
@@ -228,7 +235,7 @@
             def _():
                 @pl.loop(0, tiles)
                 def _(tile):
-                    acc[tile] += multiply(slot, tile)
+                    acc[tile] += multiply_tile(slot, tile)
 
                 pltpu.make_async_copy(wf.at[slot], w_out.at[slot], out_sem.at[slot]).start()
 
@@ -244,13 +251,13 @@
     x_got(1, 4, 5)
     take_shared()
 
-    acc[tiles] = jnp.zeros((TOK, 256), jnp.float32)
-
-    @pl.loop(0, COLS)
+    kv_acc[...] = multiply(0, FEAT, KV)
+
+    @pl.loop(1, COLS)
     def _(slot):
-        acc[tiles] += multiply(slot, tiles)
-
-    kv_buf[...] = acc[tiles].astype(jnp.bfloat16)
+        kv_acc[...] += multiply(slot, FEAT, KV)
+
+    kv_buf[...] = kv_acc[...].astype(jnp.bfloat16)
     halo = [
         move("up", kv_buf, kv_out.at[0], (next_row, col)),
         move("down", kv_buf, kv_out.at[2], (prev_row, col)),
@@ -271,20 +278,20 @@
     take_shared()
     pltpu.make_async_copy(wf.at[late_w], w_out.at[late_w], out_sem.at[late_w]).start()
 
-    @pl.loop(0, tiles)
-    def _(tile):
-        cols = pl.ds(pl.multiple_of(tile * 256, 256), 256)
-        q_buf[:, cols] = (acc[tile] + multiply(late_w, tile)).astype(jnp.bfloat16)
-        pltpu.make_async_copy(q_buf.at[:, cols], q_out.at[:, cols], q_sem.at[tile]).start()
+    for i in range(LAST):
+        cols = pl.ds(i * (FEAT // LAST), FEAT // LAST)
+        total = acc[0, :, cols] + multiply(late_w, i * (FEAT // LAST), FEAT // LAST)
+        q_buf[:, cols] = total.astype(jnp.bfloat16)
+        pltpu.make_async_copy(q_buf.at[:, cols], q_out.at[:, cols], q_sem.at[i]).start()
 
     for copy in started:
         copy.wait_send()
     for copy in halo:
         copy.wait()
     own_kv.wait()
-    for tile in range(tiles):
-        cols = pl.ds(tile * 256, 256)
-        pltpu.make_async_copy(q_buf.at[:, cols], q_out.at[:, cols], q_sem.at[tile]).wait()
+    for i in range(LAST):
+        cols = pl.ds(i * (FEAT // LAST), FEAT // LAST)
+        pltpu.make_async_copy(q_buf.at[:, cols], q_out.at[:, cols], q_sem.at[i]).wait()
     for slot in range(COLS):
         pltpu.make_async_copy(wf.at[slot], w_out.at[slot], out_sem.at[slot]).wait()
     assert len(index) <= SEMS
@@ -312,12 +319,13 @@
         scratch_shapes=[
             pltpu.VMEM((COLS, TOK, FEAT), jnp.bfloat16),
             pltpu.VMEM((COLS, FEAT, WIDE), jnp.bfloat16),
-            pltpu.VMEM((WIDE // 256, TOK, 256), jnp.float32),
+            pltpu.VMEM((FEAT // SPAN, TOK, SPAN), jnp.float32),
+            pltpu.VMEM((TOK, KV), jnp.float32),
             pltpu.VMEM((TOK, KV), jnp.bfloat16),
             pltpu.VMEM((TOK, FEAT), jnp.bfloat16),
             dma((4,)),
             dma((SEMS,)), dma((SEMS,)),
-            dma((COLS,)), dma, dma((FEAT // 256,)),
+            dma((COLS,)), dma, dma((LAST,)),
         ],
         compiler_params=pltpu.CompilerParams(
             collective_id=0, has_side_effects=True, vmem_limit_bytes=56 * MIB
@@ -331,7 +339,7 @@
 def scatter_kernel(
     dq_in, side_in, mid_in, w_in,
     out,
-    jn, wv, acc, pb, lent, far, near, pair_out, pair_in, side_got, mid, result,
+    jn, wv, acc, pb, lent, far, near, pair_out, pair_in, side_got, taken, mid, result,
     w_sem, load_sem, out_sem, send_sems, recv_sems,
 ):
     row, col, y, h, k, z, l = place()
@@ -371,15 +379,15 @@
         i = index[name]
         remote(ref, ref, send_sems.at[i], recv_sems.at[i], *l_pair).wait_recv()
 
-    send("down", side_in.at[0], side_got.at[1], (prev_row, col))
-    send("up", side_in.at[1], side_got.at[0], (next_row, col))
-
-    tiles = FEAT // 256
+    tiles = FEAT // OUT_SPAN
     low, high, both = pl.ds(0, HALF), pl.ds(HALF, HALF), pl.ds(0, TOK)
     halves = (low, high)
+    for half, rows in enumerate(halves):
+        send(("down", half), side_in.at[0, rows], side_got.at[1, rows], (prev_row, col))
+        send(("up", half), side_in.at[1, rows], side_got.at[0, rows], (next_row, col))
 
     def product(slot, tile, rows, cols):
-        tall = pl.ds(pl.multiple_of(tile * 256, 256), 256)
+        tall = pl.ds(pl.multiple_of(tile * OUT_SPAN, OUT_SPAN), OUT_SPAN)
         return lax.dot_general(
             jn[rows, cols], wv[slot, tall, cols], (((1,), (1,)), ((), ())),
             preferred_element_type=jnp.float32,
@@ -388,17 +396,20 @@
     def each_tile(step):
         @pl.loop(0, tiles)
         def _(tile):
-            step(tile, pl.ds(pl.multiple_of(tile * 256, 256), 256))
+            step(tile, pl.ds(pl.multiple_of(tile * OUT_SPAN, OUT_SPAN), OUT_SPAN))
 
     every = pl.ds(0, WIDE)
 
-    def fill(target, step, plane, rows, extra=None):
+    def fill(target, step, plane, rows, extra=None, last=None):
         slot = slot_of(step, plane)
 
         def one(tile, cols):
             value = product(slot, tile, rows, every)
             if extra is not None:
                 value += extra[:, cols].astype(jnp.float32)
+            if last is not None:
+                zeros = jnp.zeros((HALF - LEND, OUT_SPAN), jnp.float32)
+                value += jnp.concatenate([zeros, last[:, cols].astype(jnp.float32)], axis=0)
             target[rows, cols] = value.astype(jnp.bfloat16)
 
         each_tile(one)
@@ -417,6 +428,16 @@
 
             each_tile(one)
 
+    def settle(half):
+        rows = halves[half]
+        got(("down", half), side_got.at[1, rows])
+        got(("up", half), side_got.at[0, rows])
+        value = mid[rows] + side_got[0, rows].astype(jnp.float32)
+        value += side_got[1, rows].astype(jnp.float32)
+        jn[rows, FEAT:] = value.astype(jnp.bfloat16)
+
+    kept, given = pl.ds(HALF, HALF - LEND), pl.ds(TOK - LEND, LEND)
+
     def whole_part(half):
         rows = halves[half]
         for i, (step, plane) in enumerate(first):
@@ -427,27 +448,29 @@
                 pb[1, i, rows, cols] = value.astype(jnp.bfloat16)
 
             each_tile(one)
-            source = pb.at[1, i, rows]
             if i == 0:
-                send(("lend", half), source, lent.at[rows], l_pair)
-            else:
-                target = near.at[1, i - 1, rows]
-                send(("near", 1, i - 1, half), source, target, z_next if i == 1 else z_prev)
+                send(("lend", half), pb.at[1, i, rows], lent.at[rows], l_pair)
+                continue
+            rows_out = kept if half else rows
+            source, target = pb.at[1, i, rows_out], near.at[1, i - 1, rows_out]
+            send(("near", 1, i - 1, half), source, target, z_next if i == 1 else z_prev)
+        if half:
+            for way in range(2):
+                send(("give", way), pb.at[1, 1 + way, given], taken.at[way], l_pair)
 
     query_part(low)
     load_mid.wait()
-    got("down", side_got.at[1])
-    got("up", side_got.at[0])
-    jn[:, FEAT:] = (
-        mid[...] + side_got[0].astype(jnp.float32) + side_got[1].astype(jnp.float32)
-    ).astype(jnp.bfloat16)
+    settle(0)
     whole_part(0)
     query_part(high)
+    settle(1)
     whole_part(1)
 
     def near_half(way, half, extra=None):
         rows = halves[half]
-        fill(pb.at[0, 1 + way], 1 if way == 0 else 3, 0, rows, extra)
+        if half:
+            got(("give", way), taken.at[way])
+        fill(pb.at[0, 1 + way], 1 if way == 0 else 3, 0, rows, extra, taken.at[way] if half else None)
         send(
             ("near", 0, way, half), pb.at[0, 1 + way, rows], near.at[0, way, rows],
             z_next if way == 0 else z_prev,
@@ -482,13 +505,16 @@
 
     own(1)
     for half, rows in enumerate(halves):
+        rows_in = kept if half else rows
         for way in range(2):
-            got(("near", 1, way, half), near.at[1, way, rows])
+            got(("near", 1, way, half), near.at[1, way, rows_in])
 
         def pair_sum(tile, cols):
-            value = acc[1, tile, rows] + near[1, 0, rows, cols].astype(jnp.float32)
-            value += near[1, 1, rows, cols].astype(jnp.float32)
-            pair_out[rows, cols] = value.astype(jnp.bfloat16)
+            value = acc[1, tile, rows_in] + near[1, 0, rows_in, cols].astype(jnp.float32)
+            value += near[1, 1, rows_in, cols].astype(jnp.float32)
+            pair_out[rows_in, cols] = value.astype(jnp.bfloat16)
+            if half:
+                pair_out[given, cols] = acc[1, tile, given].astype(jnp.bfloat16)
 
         each_tile(pair_sum)
         send(("pair", half), pair_out.at[rows], pair_in.at[rows], l_pair)
@@ -535,7 +561,7 @@
         scratch_shapes=[
             pltpu.VMEM((TOK, WIDE), low),
             pltpu.VMEM((COLS, FEAT, WIDE), low),
-            pltpu.VMEM((3, FEAT // 256, TOK, 256), jnp.float32),
+            pltpu.VMEM((3, FEAT // OUT_SPAN, TOK, OUT_SPAN), jnp.float32),
             pltpu.VMEM((2, 3, TOK, FEAT), low),
             pltpu.VMEM((TOK, FEAT), low),
             pltpu.VMEM((2, HALF, FEAT), low),
@@ -543,10 +569,11 @@
             pltpu.VMEM((TOK, FEAT), low),
             pltpu.VMEM((TOK, FEAT), low),
             pltpu.VMEM((2, TOK, KV), low),
+            pltpu.VMEM((2, LEND, FEAT), low),
             pltpu.VMEM((TOK, KV), jnp.float32),
             pltpu.VMEM((TOK, FEAT), low),
             dma((COLS,)), dma((2,)), dma((2,)),
-            dma((16,)), dma((16,)),
+            dma((20,)), dma((20,)),
         ],
         compiler_params=pltpu.CompilerParams(
             collective_id=1, has_side_effects=True, vmem_limit_bytes=56 * MIB

time: 183 us -> 177 us (0.967)
  Pallas kernels: 179 us -> 174 us
    pallas_call x1, Pallas kernels: 74.3 us -> 71.1 us  [scatter(): pl.pallas_call(scatter_kernel, name='project_scatter', out_shape=jax.Shap...]
    pallas_call x1, Pallas kernels: 93 us -> 90.9 us  [gather(): pl.pallas_call(gather_kernel, name='gather_project', out_shape=(jax.Shape...]
where the time goes in v6:
time: 177 us
  Pallas kernels  174 us (98%)
  local copies, waits for them, and re-layouts  2.26 us (1%)
    pallas_call x1, Pallas kernels, gather(): pl.pallas_call(gather_kernel, name='gather_project', out_shape=(jax.Shape...  90.9 us
    pallas_call x1, Pallas kernels, scatter(): pl.pallas_call(scatter_kernel, name='project_scatter', out_shape=jax.Shap...  71.1 us
    pallas_call x1, Pallas kernels, attend(): pl.pallas_call(attend_kernel, name='attend', grid=(per_dev,), out_shape=(...  11.7 us

profile of v6, /device:TPU:10, one launch (start us, length us, event | category | flops | bytes accessed | tf_op | source)
XLA Modules:
  0.0 176.7 jit_solution(12067414590488125765)
XLA Ops:
  0.6 90.9 %gather_project.1 = (bf16[512,1024]{1,0:T(8,128)(2,1)}, bf16[3,512,256]{2,1,0:T(8,128)(2,1)}, bf16[8,1024,1280]{2,1,0:T(8,128)(2,1)}) custom-call(bf16[512,1024]{1,0:T(8,128)(2,1)} %x_in.1, bf16[512,1024]{1,0:T(8,128)(2,1)} %wq_in.1, bf16[512,128]{1,0:T(8,128)(2,1)} %wk_in.1, bf16[512,128]{1,0:T(8,128)(2,1)} %wv_in.1), custom_call_target="tpu_custom_call" | custom-call | flops 10737418240 | bytes 41943040 | tf_op jit(solution)/shard_map/gather_project/pallas_call | solution.py:305
  91.6 11.7 %attend.1 = (bf16[512,1024]{1,0:T(8,128)(2,1)}, bf16[512,1024]{1,0:T(8,128)(2,1)}, bf16[2,512,256]{2,1,0:T(8,128)(2,1)}, f32[512,256]{1,0:T(8,128)}) custom-call(s32[4,4]{1,0:T(4,128)} %pattern.1, s32[64]{0:T(128)} %counts.1, bf16[512,1024]{1,0:T(8,128)(2,1)} %get-tuple-element.9.q_in, bf16[512,1024]{1,0:T(8,128)(2,1)} %cot_in.1, bf16[12,128,256]{2,1,0:T(8,128)(2,1)} %bitcast.1), custom_call_target="tpu_custom_call" | custom-call | tf_op jit(solution)/shard_map/attend/pallas_call | solution.py:689
  103.3 71.1 %project_scatter.1 = bf16[512,1024]{1,0:T(8,128)(2,1)} custom-call(bf16[512,1024]{1,0:T(8,128)(2,1)} %get-tuple-element.12.dq_in, bf16[2,512,256]{2,1,0:T(8,128)(2,1)} %get-tuple-element.13.side_in, f32[512,256]{1,0:T(8,128)} %get-tuple-element.14.mid_in, bf16[8,1024,1280]{2,1,0:T(8,128)(2,1)} %get-tuple-element.15.w_in), custom_call_target="tpu_custom_call" | custom-call | flops 10737418240 | bytes 25165824 | tf_op jit(solution)/shard_map/project_scatter/pallas_call | solution.py:555
  174.5 2.3 %copy.10 = bf16[512,1024]{1,0:T(8,128)(2,1)} copy(bf16[512,1024]{1,0:T(8,128)(2,1)} %project_scatter.1) | data formatting | bytes 2097152

commit v7 on v6

--- a/solution.py
+++ b/solution.py
@@ -300,7 +300,7 @@
 SEMS = 60
 
 
-def gather(layer_input, w_query, w_key, w_value):
+def gather(*inputs):
     dma = pltpu.SemaphoreType.DMA
     return pl.pallas_call(
         gather_kernel,
@@ -328,12 +328,12 @@
             dma((COLS,)), dma, dma((LAST,)),
         ],
         compiler_params=pltpu.CompilerParams(
-            collective_id=0, has_side_effects=True, vmem_limit_bytes=56 * MIB
+            collective_id=0, has_side_effects=True, vmem_limit_bytes=40 * MIB
         ),
         cost_estimate=pl.CostEstimate(
             flops=2 * TOK * 8192 * WIDE, bytes_accessed=40 * MIB, transcendentals=0
         ),
-    )(layer_input, w_query, w_key, w_value)
+    )(*(pltpu.with_memory_space_constraint(a, pltpu.HBM) for a in inputs))
 
 
 def scatter_kernel(
@@ -576,7 +576,7 @@
             dma((20,)), dma((20,)),
         ],
         compiler_params=pltpu.CompilerParams(
-            collective_id=1, has_side_effects=True, vmem_limit_bytes=56 * MIB
+            collective_id=1, has_side_effects=True, vmem_limit_bytes=48 * MIB
         ),
         cost_estimate=pl.CostEstimate(
             flops=2 * TOK * 8192 * WIDE, bytes_accessed=24 * MIB, transcendentals=0
@@ -706,7 +706,7 @@
             pl.BlockSpec((TOK, KV), lambda b: (0, 0)),
         ),
         scratch_shapes=[pltpu.VMEM((3 * per_dev, BLOCK, KV), jnp.float32)],
-        compiler_params=pltpu.CompilerParams(vmem_limit_bytes=62 * MIB),
+        compiler_params=pltpu.CompilerParams(vmem_limit_bytes=24 * MIB),
     )(pattern, counts, query, cotangent, source.reshape(3 * per_dev, BLOCK, KV))
 
 

time: 177 us -> 173 us (0.977)
  Pallas kernels: 174 us -> 171 us
where the time goes in v7:
time: 173 us
  Pallas kernels  171 us (99%)
    pallas_call x1, Pallas kernels, gather(): pl.pallas_call(gather_kernel, name='gather_project', out_shape=(jax.Shape...  90.5 us
    pallas_call x1, Pallas kernels, scatter(): pl.pallas_call(scatter_kernel, name='project_scatter', out_shape=jax.Shap...  70.4 us
    pallas_call x1, Pallas kernels, attend(): pl.pallas_call(attend_kernel, name='attend', grid=(per_dev,), out_shape=(...  10.5 us

profile of v7, /device:TPU:10, one launch (start us, length us, event | category | flops | bytes accessed | tf_op | source)
XLA Modules:
  0.0 173.1 jit_solution(6897652591475841649)
XLA Ops:
  0.6 0.0 copy-start
  0.6 0.0 copy-start.1
  0.7 0.0 copy-start.2
  0.7 90.5 %gather_project.1 = (bf16[512,1024]{1,0:T(8,128)(2,1)S(1)}, bf16[3,512,256]{2,1,0:T(8,128)(2,1)S(1)}, bf16[8,1024,1280]{2,1,0:T(8,128)(2,1)}) custom-call(bf16[512,1024]{1,0:T(8,128)(2,1)} %x_in.1, bf16[512,1024]{1,0:T(8,128)(2,1)} %wq_in.1, bf16[512,128]{1,0:T(8,128)(2,1)} %wk_in.1, bf16[512,128]{1,0:T(8,128)(2,1)} %wv_in.1), custom_call_target="tpu_custom_call" | custom-call | flops 10737418240 | bytes 41943040 | tf_op jit(solution)/shard_map/gather_project/pallas_call | solution.py:305
  91.2 0.0 copy-done
  91.2 0.0 copy-done.1
  91.2 0.0 copy-done.2
  91.2 10.5 %attend.1 = (bf16[512,1024]{1,0:T(8,128)(2,1)}, bf16[512,1024]{1,0:T(8,128)(2,1)S(1)}, bf16[2,512,256]{2,1,0:T(8,128)(2,1)S(1)}, f32[512,256]{1,0:T(8,128)S(1)}) custom-call(s32[4,4]{1,0:T(4,128)S(1)} %copy-done.1, s32[64]{0:T(128)S(1)} %copy-done.2, bf16[512,1024]{1,0:T(8,128)(2,1)S(1)} %get-tuple-element.9.q_in, bf16[512,1024]{1,0:T(8,128)(2,1)S(1)} %copy-done, ...), custom_call_target="tpu_custom_call" | custom-call | tf_op jit(solution)/shard_map/attend/pallas_call | solution.py:689
  101.7 70.4 %project_scatter.1 = bf16[512,1024]{1,0:T(8,128)(2,1)S(1)} custom-call(bf16[512,1024]{1,0:T(8,128)(2,1)S(1)} %get-tuple-element.12.dq_in, bf16[2,512,256]{2,1,0:T(8,128)(2,1)S(1)} %get-tuple-element.13.side_in, f32[512,256]{1,0:T(8,128)S(1)} %get-tuple-element.14.mid_in, bf16[8,1024,1280]{2,1,0:T(8,128)(2,1)} %get-tuple-element.15.w_in), custom_call_target="tpu_custom_call" | custom-call | flops 10737418240 | bytes 25165824 | tf_op jit(solution)/shard_map/project_scatter/pallas_call | solution.py:555
  172.1 1.0 copy.10
Async XLA Ops:
  0.6 90.6 %copy-start = (bf16[512,1024]{1,0:T(8,128)(2,1)S(1)}, bf16[512,1024]{1,0:T(8,128)(2,1)}, u32[]{:S(2)}) copy-start(bf16[512,1024]{1,0:T(8,128)(2,1)} %cot_in.1) | copy-start | bytes 3145732
  0.6 90.6 %copy-start.1 = (s32[4,4]{1,0:T(4,128)S(1)}, s32[4,4]{1,0:T(4,128)}, u32[]{:S(2)}) copy-start(s32[4,4]{1,0:T(4,128)} %pattern.1) | copy-start | bytes 196
  0.7 90.6 %copy-start.2 = (s32[64]{0:T(128)S(1)}, s32[64]{0:T(128)}, u32[]{:S(2)}) copy-start(s32[64]{0:T(128)} %counts.1) | copy-start | bytes 772

commit v8 on v7

--- a/solution.py
+++ b/solution.py
@@ -22,7 +22,7 @@
 MESH = pl.DeviceIdType.MESH
 SPAN = 1024
 LAST = 2
-LEND = 64
+LEND = 96
 OUT_SPAN = 1024
 MIB = 1024 * 1024
 LOG2E = 1.4426950408889634
@@ -382,9 +382,11 @@
     tiles = FEAT // OUT_SPAN
     low, high, both = pl.ds(0, HALF), pl.ds(HALF, HALF), pl.ds(0, TOK)
     halves = (low, high)
-    for half, rows in enumerate(halves):
-        send(("down", half), side_in.at[0, rows], side_got.at[1, rows], (prev_row, col))
-        send(("up", half), side_in.at[1, rows], side_got.at[0, rows], (next_row, col))
+    pieces = (pl.ds(0, HALF // 2), pl.ds(HALF // 2, HALF // 2), high)
+    pieces_of = ((0, 1), (2,))
+    for i, rows in enumerate(pieces):
+        send(("down", i), side_in.at[0, rows], side_got.at[1, rows], (prev_row, col))
+        send(("up", i), side_in.at[1, rows], side_got.at[0, rows], (next_row, col))
 
     def product(slot, tile, rows, cols):
         tall = pl.ds(pl.multiple_of(tile * OUT_SPAN, OUT_SPAN), OUT_SPAN)
@@ -428,20 +430,20 @@
 
             each_tile(one)
 
-    def settle(half):
-        rows = halves[half]
-        got(("down", half), side_got.at[1, rows])
-        got(("up", half), side_got.at[0, rows])
+    def settle(piece):
+        rows = pieces[piece]
+        got(("down", piece), side_got.at[1, rows])
+        got(("up", piece), side_got.at[0, rows])
         value = mid[rows] + side_got[0, rows].astype(jnp.float32)
         value += side_got[1, rows].astype(jnp.float32)
         jn[rows, FEAT:] = value.astype(jnp.bfloat16)
 
     kept, given = pl.ds(HALF, HALF - LEND), pl.ds(TOK - LEND, LEND)
 
-    def whole_part(half):
-        rows = halves[half]
-        for i, (step, plane) in enumerate(first):
-            slot = slot_of(step, plane)
+    def whole_part(piece):
+        rows = pieces[piece]
+        for i in (1, 2, 0):
+            slot = slot_of(*first[i])
 
             def one(tile, cols):
                 value = acc[i, tile, rows] + product(slot, tile, rows, pl.ds(FEAT, KV))
@@ -449,22 +451,24 @@
 
             each_tile(one)
             if i == 0:
-                send(("lend", half), pb.at[1, i, rows], lent.at[rows], l_pair)
+                send(("lend", piece), pb.at[1, i, rows], lent.at[rows], l_pair)
                 continue
-            rows_out = kept if half else rows
+            rows_out = kept if piece == 2 else rows
             source, target = pb.at[1, i, rows_out], near.at[1, i - 1, rows_out]
-            send(("near", 1, i - 1, half), source, target, z_next if i == 1 else z_prev)
-        if half:
+            send(("near", 1, i - 1, piece), source, target, z_next if i == 1 else z_prev)
+        if piece == 2:
             for way in range(2):
                 send(("give", way), pb.at[1, 1 + way, given], taken.at[way], l_pair)
 
     query_part(low)
     load_mid.wait()
-    settle(0)
-    whole_part(0)
+    for piece in pieces_of[0]:
+        settle(piece)
+        whole_part(piece)
     query_part(high)
-    settle(1)
-    whole_part(1)
+    for piece in pieces_of[1]:
+        settle(piece)
+        whole_part(piece)
 
     def near_half(way, half, extra=None):
         rows = halves[half]
@@ -478,7 +482,8 @@
 
     loads[2, 0].wait()
     for half, rows in enumerate(halves):
-        got(("lend", half), lent.at[rows])
+        for piece in pieces_of[half]:
+            got(("lend", piece), lent.at[pieces[piece]])
         fill(pb.at[0, 0], 2, 0, rows, lent.at[rows])
         send(("far", half), pb.at[0, 0, rows], far.at[half], z_prev if half else z_next)
     loads[1, 0].wait()
@@ -507,7 +512,8 @@
     for half, rows in enumerate(halves):
         rows_in = kept if half else rows
         for way in range(2):
-            got(("near", 1, way, half), near.at[1, way, rows_in])
+            for piece in pieces_of[half]:
+                got(("near", 1, way, piece), near.at[1, way, rows_in if half else pieces[piece]])
 
         def pair_sum(tile, cols):
             value = acc[1, tile, rows_in] + near[1, 0, rows_in, cols].astype(jnp.float32)
@@ -573,7 +579,7 @@
             pltpu.VMEM((TOK, KV), jnp.float32),
             pltpu.VMEM((TOK, FEAT), low),
             dma((COLS,)), dma((2,)), dma((2,)),
-            dma((20,)), dma((20,)),
+            dma((25,)), dma((25,)),
         ],
         compiler_params=pltpu.CompilerParams(
             collective_id=1, has_side_effects=True, vmem_limit_bytes=48 * MIB
@@ -587,9 +593,8 @@
 def attend_kernel(
     pattern, counts, q_in, cot_in, kv_in,
     out, dq_out, side_out, mid_out,
-    owed,
+    owed, held, out_sem,
 ):
-    block = pl.program_id(0)
     per_dev = TOK // BLOCK
     block_count = ROWS * per_dev
     first = lax.axis_index("row") * per_dev
@@ -597,115 +602,118 @@
     exponent_scale = scale * LOG2E
     pair = 2 * HEAD_DIM
 
-    @pl.when(block == 0)
-    def _():
-        owed[...] = jnp.zeros_like(owed)
-
-    chosen = [pattern[block, i] for i in range(4)]
-    local = [(b - first + per_dev + block_count) % block_count for b in chosen]
-    keys = jnp.concatenate([kv_in[i, :, :HEAD_DIM] for i in local], axis=0)
-    values = jnp.concatenate([kv_in[i, :, HEAD_DIM:] for i in local], axis=0)
-    keys_t, values_t = keys.T, values.T
-    spot = lax.broadcasted_iota(jnp.int32, (BLOCK, pair), 0)
-    live = jnp.concatenate([spot < counts[b] for b in chosen], axis=0)
-    own_count = counts[first + block]
-    lane = lax.broadcasted_iota(jnp.int32, (1, pair), 1)
-    query_live = jnp.where(lane % BLOCK < own_count, 1.0, 0.0)
-    row_live = lax.broadcasted_iota(jnp.int32, (BLOCK, HEAD_DIM), 0) < own_count
-    row_live = jnp.where(row_live, 1.0, 0.0).astype(jnp.bfloat16)
-
-    def heads(ref, start, mask=None):
-        parts = [ref[:, start + i * HEAD_DIM : start + (i + 1) * HEAD_DIM] for i in range(2)]
-        if mask is not None:
-            parts = [part * mask for part in parts]
-        return jnp.concatenate(parts, axis=0)
-
-    def dot(a, b, dims):
-        return lax.dot_general(a, b, (dims, ((), ())), preferred_element_type=jnp.float32)
-
-    def put(ref, start, both):
-        low = both.astype(jnp.bfloat16)
-        for i in range(2):
-            cols = slice(start + i * HEAD_DIM, start + (i + 1) * HEAD_DIM)
-            ref[:, cols] = low[:, i * HEAD_DIM : (i + 1) * HEAD_DIM].T
-
-    def begin(start):
-        query = heads(q_in, start)
-        grad_out = heads(cot_in, start, row_live)
-        raw = dot(keys, query, ((1,), (1,)))
-        return start, query, grad_out, raw, dot(values, grad_out, ((1,), (1,)))
-
-    def middle(start, query, grad_out, raw, grad_probs):
-        raw = jnp.where(live, raw, -1e30)
-        top = jnp.max(raw, axis=0, keepdims=True)
-        power = jnp.exp2((raw - top) * exponent_scale)
-        probs = power * (1.0 / jnp.sum(power, axis=0, keepdims=True))
-        probs_low = probs.astype(jnp.bfloat16)
-        delta = jnp.sum(probs_low.astype(jnp.float32) * grad_probs, axis=0, keepdims=True)
-        grad_scores = (probs * (grad_probs - delta) * scale).astype(jnp.bfloat16)
-        return start, query, grad_out, probs_low, grad_scores
-
-    def end(start, query, grad_out, probs_low, grad_scores):
-        put(out, start, dot(values_t, probs_low, ((1,), (0,))) * query_live)
-        put(dq_out, start, dot(keys_t, grad_scores, ((1,), (0,))))
-        key_part = dot(grad_scores, query, ((1,), (0,)))
-        value_part = dot(probs_low, grad_out, ((1,), (0,)))
-        return key_part, value_part
-
-    starts = range(0, FEAT, pair)
-    parts = []
-    coming, going = begin(starts[0]), None
-    for i in range(len(starts)):
-        now = coming
-        if i + 1 < len(starts):
-            coming = begin(starts[i + 1])
-        done = middle(*now)
-        if going is not None:
-            parts.append(end(*going))
-        going = done
-    parts.append(end(*going))
-    grad_keys = sum(part[0] for part in parts[1:]) + parts[0][0]
-    grad_values = sum(part[1] for part in parts[1:]) + parts[0][1]
-
-    for i, spot in enumerate(local):
+    owed[...] = jnp.zeros_like(owed)
+
+    def copy_out(block):
+        rows = pl.ds(block * BLOCK, BLOCK)
+        return pltpu.make_async_copy(held.at[rows], out.at[rows], out_sem.at[block])
+
+    @pl.loop(0, per_dev)
+    def _(block):
+        block_rows = pl.ds(pl.multiple_of(block * BLOCK, BLOCK), BLOCK)
+        chosen = [pattern[block, i] for i in range(4)]
+        local = [(b - first + per_dev + block_count) % block_count for b in chosen]
+        keys = jnp.concatenate([kv_in[i, :, :HEAD_DIM] for i in local], axis=0)
+        values = jnp.concatenate([kv_in[i, :, HEAD_DIM:] for i in local], axis=0)
+        keys_t, values_t = keys.T, values.T
+        spot = lax.broadcasted_iota(jnp.int32, (BLOCK, pair), 0)
+        live = jnp.concatenate([spot < counts[b] for b in chosen], axis=0)
+        own_count = counts[first + block]
+        lane = lax.broadcasted_iota(jnp.int32, (1, pair), 1)
+        query_live = jnp.where(lane % BLOCK < own_count, 1.0, 0.0)
+        row_live = lax.broadcasted_iota(jnp.int32, (BLOCK, HEAD_DIM), 0) < own_count
+        row_live = jnp.where(row_live, 1.0, 0.0).astype(jnp.bfloat16)
+
+        def heads(ref, start, mask=None):
+            parts = [ref[block_rows, start + i * HEAD_DIM : start + (i + 1) * HEAD_DIM] for i in range(2)]
+            if mask is not None:
+                parts = [part * mask for part in parts]
+            return jnp.concatenate(parts, axis=0)
+
+        def dot(a, b, dims):
+            return lax.dot_general(a, b, (dims, ((), ())), preferred_element_type=jnp.float32)
+
+        def put(ref, start, both):
+            low = both.astype(jnp.bfloat16)
+            for i in range(2):
+                cols = slice(start + i * HEAD_DIM, start + (i + 1) * HEAD_DIM)
+                ref[block_rows, cols] = low[:, i * HEAD_DIM : (i + 1) * HEAD_DIM].T
+
+        def begin(start):
+            query = heads(q_in, start)
+            grad_out = heads(cot_in, start, row_live)
+            raw = dot(keys, query, ((1,), (1,)))
+            return start, query, grad_out, raw, dot(values, grad_out, ((1,), (1,)))
+
+        def middle(start, query, grad_out, raw, grad_probs):
+            raw = jnp.where(live, raw, -1e30)
+            top = jnp.max(raw, axis=0, keepdims=True)
+            power = jnp.exp2((raw - top) * exponent_scale)
+            probs = power * (1.0 / jnp.sum(power, axis=0, keepdims=True))
+            probs_low = probs.astype(jnp.bfloat16)
+            delta = jnp.sum(probs_low.astype(jnp.float32) * grad_probs, axis=0, keepdims=True)
+            grad_scores = (probs * (grad_probs - delta) * scale).astype(jnp.bfloat16)
+            return start, query, grad_out, probs_low, grad_scores
+
+        def end(start, query, grad_out, probs_low, grad_scores):
+            put(held, start, dot(values_t, probs_low, ((1,), (0,))) * query_live)
+            put(dq_out, start, dot(keys_t, grad_scores, ((1,), (0,))))
+            key_part = dot(grad_scores, query, ((1,), (0,)))
+            value_part = dot(probs_low, grad_out, ((1,), (0,)))
+            return key_part, value_part
+
+        starts = range(0, FEAT, pair)
+        parts = []
+        coming, going = begin(starts[0]), None
+        for i in range(len(starts)):
+            now = coming
+            if i + 1 < len(starts):
+                coming = begin(starts[i + 1])
+            done = middle(*now)
+            if going is not None:
+                parts.append(end(*going))
+            going = done
+        parts.append(end(*going))
+        grad_keys = sum(part[0] for part in parts[1:]) + parts[0][0]
+        grad_values = sum(part[1] for part in parts[1:]) + parts[0][1]
+
+        for i, spot in enumerate(local):
+            rows = slice(i * BLOCK, (i + 1) * BLOCK)
+            owed[spot, :, :HEAD_DIM] += grad_keys[rows]
+            owed[spot, :, HEAD_DIM:] += grad_values[rows]
+
+        copy_out(block).start()
+
+    for i in range(per_dev):
         rows = slice(i * BLOCK, (i + 1) * BLOCK)
-        owed[spot, :, :HEAD_DIM] += grad_keys[rows]
-        owed[spot, :, HEAD_DIM:] += grad_values[rows]
-
-    @pl.when(block == per_dev - 1)
-    def _():
-        for i in range(per_dev):
-            rows = slice(i * BLOCK, (i + 1) * BLOCK)
-            side_out[0, rows] = owed[i].astype(jnp.bfloat16)
-            mid_out[rows] = owed[per_dev + i]
-            side_out[1, rows] = owed[2 * per_dev + i].astype(jnp.bfloat16)
+        side_out[0, rows] = owed[i].astype(jnp.bfloat16)
+        mid_out[rows] = owed[per_dev + i]
+        side_out[1, rows] = owed[2 * per_dev + i].astype(jnp.bfloat16)
+    for block in range(per_dev):
+        copy_out(block).wait()
 
 
 def attend(pattern, counts, query, cotangent, source):
     per_dev = TOK // BLOCK
-    tokens = pl.BlockSpec((BLOCK, FEAT), lambda b: (b, 0))
+    vmem = pl.BlockSpec(memory_space=pltpu.VMEM)
     smem = pl.BlockSpec(memory_space=pltpu.SMEM)
     low = jnp.bfloat16
     return pl.pallas_call(
         attend_kernel,
         name="attend",
-        grid=(per_dev,),
         out_shape=(
             jax.ShapeDtypeStruct((TOK, FEAT), low),
             jax.ShapeDtypeStruct((TOK, FEAT), low),
             jax.ShapeDtypeStruct((2, TOK, KV), low),
             jax.ShapeDtypeStruct((TOK, KV), jnp.float32),
         ),
-        in_specs=[
-            smem, smem, tokens, tokens,
-            pl.BlockSpec((3 * per_dev, BLOCK, KV), lambda b: (0, 0, 0)),
+        in_specs=[smem, smem, vmem, vmem, vmem],
+        out_specs=(pl.BlockSpec(memory_space=pl.ANY), vmem, vmem, vmem),
+        scratch_shapes=[
+            pltpu.VMEM((3 * per_dev, BLOCK, KV), jnp.float32),
+            pltpu.VMEM((TOK, FEAT), low),
+            pltpu.SemaphoreType.DMA((per_dev,)),
         ],
-        out_specs=(
-            tokens, tokens,
-            pl.BlockSpec((2, TOK, KV), lambda b: (0, 0, 0)),
-            pl.BlockSpec((TOK, KV), lambda b: (0, 0)),
-        ),
-        scratch_shapes=[pltpu.VMEM((3 * per_dev, BLOCK, KV), jnp.float32)],
         compiler_params=pltpu.CompilerParams(vmem_limit_bytes=24 * MIB),
     )(pattern, counts, query, cotangent, source.reshape(3 * per_dev, BLOCK, KV))
 

time: 173 us -> 173 us (level)
  no operation moved by 1% of the time
where the time goes in v8:
time: 173 us; the launch traced here: 172 us
  Pallas kernels  171 us (99%)
    pallas_call x1, Pallas kernels, gather(): pl.pallas_call(gather_kernel, name='gather_project', out_shape=(jax.Shape...  90.5 us
    pallas_call x1, Pallas kernels, scatter(): pl.pallas_call(scatter_kernel, name='project_scatter', out_shape=jax.Shap...  69.8 us
    pallas_call x1, Pallas kernels, attend(): pl.pallas_call(attend_kernel, name='attend', out_shape=(jax.ShapeDtypeStr...  10.3 us

profile of v8, /device:TPU:10, one launch (start us, length us, event | category | flops | bytes accessed | tf_op | source)
XLA Modules:
  0.0 172.3 jit_solution(6411157119036965451)
XLA Ops:
  0.6 0.0 copy-start
  0.6 0.0 copy-start.1
  0.7 0.0 copy-start.2
  0.7 90.5 %gather_project.1 = (bf16[512,1024]{1,0:T(8,128)(2,1)S(1)}, bf16[3,512,256]{2,1,0:T(8,128)(2,1)S(1)}, bf16[8,1024,1280]{2,1,0:T(8,128)(2,1)}) custom-call(bf16[512,1024]{1,0:T(8,128)(2,1)} %x_in.1, bf16[512,1024]{1,0:T(8,128)(2,1)} %wq_in.1, bf16[512,128]{1,0:T(8,128)(2,1)} %wk_in.1, bf16[512,128]{1,0:T(8,128)(2,1)} %wv_in.1), custom_call_target="tpu_custom_call" | custom-call | flops 10737418240 | bytes 41943040 | tf_op jit(solution)/shard_map/gather_project/pallas_call | solution.py:305
  91.2 0.0 copy-done
  91.2 0.0 copy-done.1
  91.2 0.0 copy-done.2
  91.2 10.3 %attend.1 = (bf16[512,1024]{1,0:T(8,128)(2,1)}, bf16[512,1024]{1,0:T(8,128)(2,1)S(1)}, bf16[2,512,256]{2,1,0:T(8,128)(2,1)S(1)}, f32[512,256]{1,0:T(8,128)S(1)}) custom-call(s32[4,4]{1,0:T(4,128)S(1)} %copy-done.1, s32[64]{0:T(128)S(1)} %copy-done.2, bf16[512,1024]{1,0:T(8,128)(2,1)S(1)} %get-tuple-element.9.q_in, bf16[512,1024]{1,0:T(8,128)(2,1)S(1)} %copy-done, ...), custom_call_target="tpu_custom_call" | custom-call | tf_op jit(solution)/shard_map/attend/pallas_call | solution.py:701
  101.5 69.8 %project_scatter.1 = bf16[512,1024]{1,0:T(8,128)(2,1)S(1)} custom-call(bf16[512,1024]{1,0:T(8,128)(2,1)S(1)} %get-tuple-element.12.dq_in, bf16[2,512,256]{2,1,0:T(8,128)(2,1)S(1)} %get-tuple-element.13.side_in, f32[512,256]{1,0:T(8,128)S(1)} %get-tuple-element.14.mid_in, bf16[8,1024,1280]{2,1,0:T(8,128)(2,1)} %get-tuple-element.15.w_in), custom_call_target="tpu_custom_call" | custom-call | flops 10737418240 | bytes 25165824 | tf_op jit(solution)/shard_map/project_scatter/pallas_call | solution.py:561
  171.3 1.0 copy.10
Async XLA Ops:
  0.6 90.6 %copy-start = (bf16[512,1024]{1,0:T(8,128)(2,1)S(1)}, bf16[512,1024]{1,0:T(8,128)(2,1)}, u32[]{:S(2)}) copy-start(bf16[512,1024]{1,0:T(8,128)(2,1)} %cot_in.1) | copy-start | bytes 3145732
  0.6 90.6 %copy-start.1 = (s32[4,4]{1,0:T(4,128)S(1)}, s32[4,4]{1,0:T(4,128)}, u32[]{:S(2)}) copy-start(s32[4,4]{1,0:T(4,128)} %pattern.1) | copy-start | bytes 196
  0.7 90.6 %copy-start.2 = (s32[64]{0:T(128)S(1)}, s32[64]{0:T(128)}, u32[]{:S(2)}) copy-start(s32[64]{0:T(128)} %counts.1) | copy-start | bytes 772

commit v9 on v8

--- a/solution.py
+++ b/solution.py
@@ -608,7 +608,7 @@
         rows = pl.ds(block * BLOCK, BLOCK)
         return pltpu.make_async_copy(held.at[rows], out.at[rows], out_sem.at[block])
 
-    @pl.loop(0, per_dev)
+    @pl.loop(0, per_dev, unroll=True)
     def _(block):
         block_rows = pl.ds(pl.multiple_of(block * BLOCK, BLOCK), BLOCK)
         chosen = [pattern[block, i] for i in range(4)]

time: 173 us -> 173 us (level)
  no operation moved by 1% of the time
where the time goes in v9:
time: 173 us; the launch traced here: 172 us
  Pallas kernels  170 us (98%)
    pallas_call x1, Pallas kernels, gather(): pl.pallas_call(gather_kernel, name='gather_project', out_shape=(jax.Shape...  90.7 us
    pallas_call x1, Pallas kernels, scatter(): pl.pallas_call(scatter_kernel, name='project_scatter', out_shape=jax.Shap...  69.9 us
    pallas_call x1, Pallas kernels, attend(): pl.pallas_call(attend_kernel, name='attend', out_shape=(jax.ShapeDtypeStr...  9.73 us

profile of v9, /device:TPU:10, one launch (start us, length us, event | category | flops | bytes accessed | tf_op | source)
XLA Modules:
  0.0 172.0 jit_solution(15599782982144145975)
XLA Ops:
  0.6 0.0 copy-start
  0.6 0.0 copy-start.1
  0.7 0.0 copy-start.2
  0.7 90.7 %gather_project.1 = (bf16[512,1024]{1,0:T(8,128)(2,1)S(1)}, bf16[3,512,256]{2,1,0:T(8,128)(2,1)S(1)}, bf16[8,1024,1280]{2,1,0:T(8,128)(2,1)}) custom-call(bf16[512,1024]{1,0:T(8,128)(2,1)} %x_in.1, bf16[512,1024]{1,0:T(8,128)(2,1)} %wq_in.1, bf16[512,128]{1,0:T(8,128)(2,1)} %wk_in.1, bf16[512,128]{1,0:T(8,128)(2,1)} %wv_in.1), custom_call_target="tpu_custom_call" | custom-call | flops 10737418240 | bytes 41943040 | tf_op jit(solution)/shard_map/gather_project/pallas_call | solution.py:305
  91.4 0.0 copy-done
  91.4 0.0 copy-done.1
  91.4 0.0 copy-done.2
  91.4 9.7 %attend.1 = (bf16[512,1024]{1,0:T(8,128)(2,1)}, bf16[512,1024]{1,0:T(8,128)(2,1)S(1)}, bf16[2,512,256]{2,1,0:T(8,128)(2,1)S(1)}, f32[512,256]{1,0:T(8,128)S(1)}) custom-call(s32[4,4]{1,0:T(4,128)S(1)} %copy-done.1, s32[64]{0:T(128)S(1)} %copy-done.2, bf16[512,1024]{1,0:T(8,128)(2,1)S(1)} %get-tuple-element.9.q_in, bf16[512,1024]{1,0:T(8,128)(2,1)S(1)} %copy-done, ...), custom_call_target="tpu_custom_call" | custom-call | tf_op jit(solution)/shard_map/attend/pallas_call | solution.py:701
  101.1 69.9 %project_scatter.1 = bf16[512,1024]{1,0:T(8,128)(2,1)S(1)} custom-call(bf16[512,1024]{1,0:T(8,128)(2,1)S(1)} %get-tuple-element.12.dq_in, bf16[2,512,256]{2,1,0:T(8,128)(2,1)S(1)} %get-tuple-element.13.side_in, f32[512,256]{1,0:T(8,128)S(1)} %get-tuple-element.14.mid_in, bf16[8,1024,1280]{2,1,0:T(8,128)(2,1)} %get-tuple-element.15.w_in), custom_call_target="tpu_custom_call" | custom-call | flops 10737418240 | bytes 25165824 | tf_op jit(solution)/shard_map/project_scatter/pallas_call | solution.py:561
  171.0 1.0 copy.10
Async XLA Ops:
  0.6 90.7 %copy-start = (bf16[512,1024]{1,0:T(8,128)(2,1)S(1)}, bf16[512,1024]{1,0:T(8,128)(2,1)}, u32[]{:S(2)}) copy-start(bf16[512,1024]{1,0:T(8,128)(2,1)} %cot_in.1) | copy-start | bytes 3145732
  0.6 90.7 %copy-start.1 = (s32[4,4]{1,0:T(4,128)S(1)}, s32[4,4]{1,0:T(4,128)}, u32[]{:S(2)}) copy-start(s32[4,4]{1,0:T(4,128)} %pattern.1) | copy-start | bytes 196
  0.7 90.7 %copy-start.2 = (s32[64]{0:T(128)S(1)}, s32[64]{0:T(128)}, u32[]{:S(2)}) copy-start(s32[64]{0:T(128)} %counts.1) | copy-start | bytes 772
